TPU v7x, 32 devices: a whole 2x2x4 slice. The times are simulated.
32 devices in a mesh: seq: 4 (over x, core), fsdp: 8 (over z, y).
Axes of the slice: x: 2, y: 2, z: 4, core: 2. Of those that a mesh axis runs over, the one named last changes fastest.
Arguments:
- layer_input: bfloat16 [8, 1536, 1024], P('fsdp', 'seq'), may hold values from -12 to 12
- query_weight: bfloat16 [1024, 1024], P('fsdp'), may hold values from -0.1875 to 0.1875
- key_weight: bfloat16 [1024, 1024], P('fsdp'), may hold values from -0.1875 to 0.1875
- value_weight: bfloat16 [1024, 1024], P('fsdp'), may hold values from -0.1875 to 0.1875
- output_weight: bfloat16 [1024, 1024], P('fsdp'), may hold values from -0.75 to 0.75
- query_bias: bfloat16 [1024], P('fsdp'), may hold values from -4 to 4
- value_bias: bfloat16 [1024], P('fsdp'), may hold values from -1.5 to 1.5
- output_bias: bfloat16 [1024], P('fsdp'), may hold values from -4 to 4
- attn_gain: bfloat16 [1024], P('fsdp'), may hold values from 0.5 to 1.5
- attn_shift: bfloat16 [1024], P('fsdp'), may hold values from -4 to 4
- in_weight: bfloat16 [1024, 4096], P('fsdp'), may hold values from -0.1875 to 0.1875
- in_bias: bfloat16 [4096], P('fsdp'), may hold values from -4 to 4
- out_weight: bfloat16 [4096, 1024], P('fsdp'), may hold values from -0.09375 to 0.09375
- out_bias: bfloat16 [1024], P('fsdp'), may hold values from -4 to 4
- out_gain: bfloat16 [1024], P('fsdp'), may hold values from 0.5 to 1.5
- out_shift: bfloat16 [1024], P('fsdp'), may hold values from -4 to 4
- out_cotangent: bfloat16 [8, 1536, 1024], P('fsdp', 'seq'), may hold values from -6 to 6
Outputs:
- layer_output: bfloat16 [8, 1536, 1024], P('fsdp', 'seq')
- input_grad: float32 [8, 1536, 1024], P('fsdp', 'seq')
- query_weight_grad: float32 [1024, 1024], P('fsdp')
- key_weight_grad: float32 [1024, 1024], P('fsdp')
- value_weight_grad: float32 [1024, 1024], P('fsdp')
- output_weight_grad: float32 [1024, 1024], P('fsdp')
- query_bias_grad: float32 [1024], P('fsdp')
- value_bias_grad: float32 [1024], P('fsdp')
- output_bias_grad: float32 [1024], P('fsdp')
- attn_gain_grad: float32 [1024], P('fsdp')
- attn_shift_grad: float32 [1024], P('fsdp')
- in_weight_grad: float32 [1024, 4096], P('fsdp')
- in_bias_grad: float32 [4096], P('fsdp')
- out_weight_grad: float32 [4096, 1024], P('fsdp')
- out_bias_grad: float32 [1024], P('fsdp')
- out_gain_grad: float32 [1024], P('fsdp')
- out_shift_grad: float32 [1024], P('fsdp')
- rms_values: float32 [5], replicated
All inputs are finite; a program needn't handle non-finite values.
Results may differ from a plain program's by a relative error of at most 0.015.
Values may be sent and summed in bfloat16 or wider, within the bound.
A program may use at most 192 MiB of HBM per device.

v0:
```python
import jax
import jax.numpy as jnp
from jax import lax
from jax.sharding import PartitionSpec as P

HD = 64


def layer_norm(stream, gain, shift):
    centre = stream - jnp.mean(stream, axis=-1, keepdims=True)
    variance = jnp.mean(centre * centre, axis=-1, keepdims=True)
    return centre * lax.rsqrt(variance + 1e-05) * gain + shift


def gelu_exact(inputs):
    return jax.nn.gelu(inputs, approximate=False)


def column_sums(matrix):
    return jnp.sum(matrix.astype(jnp.float32), axis=0)


def local(
    layer_input,
    query_weight,
    key_weight,
    value_weight,
    output_weight,
    query_bias,
    value_bias,
    output_bias,
    attn_gain,
    attn_shift,
    in_weight,
    in_bias,
    out_weight,
    out_bias,
    out_gain,
    out_shift,
    out_cotangent,
):
    half = jnp.bfloat16
    single = jnp.float32
    fsdp_count = lax.axis_size("fsdp")
    seq_count = lax.axis_size("seq")
    (
        full_query,
        full_key,
        full_value,
        full_output,
        bias_query,
        bias_value,
        bias_output,
        gain_one,
        shift_one,
    ) = (
        lax.all_gather(query_weight, "fsdp", axis=0, tiled=True),
        lax.all_gather(key_weight, "fsdp", axis=0, tiled=True),
        lax.all_gather(value_weight, "fsdp", axis=0, tiled=True),
        lax.all_gather(output_weight, "fsdp", axis=0, tiled=True),
        lax.all_gather(query_bias, "fsdp", axis=0, tiled=True),
        lax.all_gather(value_bias, "fsdp", axis=0, tiled=True),
        lax.all_gather(output_bias, "fsdp", axis=0, tiled=True),
        lax.all_gather(attn_gain, "fsdp", axis=0, tiled=True),
        lax.all_gather(attn_shift, "fsdp", axis=0, tiled=True),
    )
    full_in, full_out, bias_in, bias_out, gain_two, shift_two = (
        lax.all_gather(in_weight, "fsdp", axis=0, tiled=True),
        lax.all_gather(out_weight, "fsdp", axis=0, tiled=True),
        lax.all_gather(in_bias, "fsdp", axis=0, tiled=True),
        lax.all_gather(out_bias, "fsdp", axis=0, tiled=True),
        lax.all_gather(out_gain, "fsdp", axis=0, tiled=True),
        lax.all_gather(out_shift, "fsdp", axis=0, tiled=True),
    )
    model_width = layer_input.shape[-1]
    tokens = layer_input.reshape(-1, model_width)
    token_rows = tokens.shape[0]
    tokens_single = tokens.astype(single)
    query_rows = (
        jnp.dot(tokens, full_query, preferred_element_type=single) + bias_query.astype(single)
    ).astype(half)
    key_rows = jnp.dot(tokens, full_key, preferred_element_type=single).astype(half)
    value_rows = (
        jnp.dot(tokens, full_value, preferred_element_type=single) + bias_value.astype(single)
    ).astype(half)
    stacked = jnp.stack([query_rows, key_rows, value_rows])
    regrouped = lax.all_to_all(stacked, "seq", split_axis=2, concat_axis=1, tiled=True)
    seq_length = regrouped.shape[1]
    local_width = regrouped.shape[2]
    heads_here = local_width // HD
    query_heads = regrouped[0].reshape(seq_length, heads_here, HD)
    key_heads = regrouped[1].reshape(seq_length, heads_here, HD)
    value_heads = regrouped[2].reshape(seq_length, heads_here, HD)
    block_rows = min(512, seq_length)
    block_count = seq_length // block_rows
    query_blocks = query_heads.reshape(block_count, block_rows, heads_here, HD)

    def forward_block(query_block):
        scores = (
            jnp.einsum("qhd,khd->hqk", query_block, key_heads, preferred_element_type=single)
            * 0.125
        )
        row_max = jnp.max(scores, axis=-1, keepdims=True)
        exp_scores = jnp.exp(scores - row_max)
        row_total = jnp.sum(exp_scores, axis=-1, keepdims=True)
        attn_probs = exp_scores / row_total
        block_out = jnp.einsum(
            "hqk,khd->qhd", attn_probs.astype(half), value_heads, preferred_element_type=single
        )
        return (block_out.astype(half), row_max[..., 0] + jnp.log(row_total[..., 0]))

    mixed_blocks, log_total = lax.map(forward_block, query_blocks)
    attn_mixed = mixed_blocks.reshape(seq_length, local_width)
    regathered = lax.all_to_all(attn_mixed, "seq", split_axis=0, concat_axis=1, tiled=True)
    attn_out = jnp.dot(regathered, full_output, preferred_element_type=single) + bias_output.astype(
        single
    )
    normed, pull_first = jax.vjp(
        layer_norm, tokens_single + attn_out, gain_one.astype(single), shift_one.astype(single)
    )
    normed_low = normed.astype(half)
    hidden_pre = jnp.dot(normed_low, full_in, preferred_element_type=single) + bias_in.astype(
        single
    )
    hidden_single, pull_gelu = jax.vjp(gelu_exact, hidden_pre)
    hidden = hidden_single.astype(half)
    branch = jnp.dot(hidden, full_out, preferred_element_type=single) + bias_out.astype(single)
    layer_out, pull_second = jax.vjp(
        layer_norm, normed + branch, gain_two.astype(single), shift_two.astype(single)
    )
    squares = jnp.stack(
        [
            jnp.sum(tokens_single * tokens_single),
            jnp.sum(attn_out * attn_out),
            jnp.sum(normed * normed),
            jnp.sum(branch * branch),
            jnp.sum(layer_out * layer_out),
        ]
    )
    square_sums = lax.psum(squares, ("seq", "fsdp"))
    rms_values = jnp.sqrt(square_sums / single(token_rows * model_width * seq_count * fsdp_count))
    cotangent = out_cotangent.reshape(token_rows, model_width).astype(single)
    grad_stream, grad_gain_two, grad_shift_two = pull_second(cotangent)
    grad_branch = grad_stream.astype(half)
    grad_bias_out = column_sums(grad_branch)
    grad_out = jnp.dot(hidden.T, grad_branch, preferred_element_type=single)
    grad_hidden = jnp.dot(grad_branch, full_out.T, preferred_element_type=single)
    grad_pre = pull_gelu(grad_hidden)[0].astype(half)
    grad_bias_in = column_sums(grad_pre)
    grad_in = jnp.dot(normed_low.T, grad_pre, preferred_element_type=single)
    grad_normed = grad_stream + jnp.dot(grad_pre, full_in.T, preferred_element_type=single)
    grad_h, grad_gain_one, grad_shift_one = pull_first(grad_normed)
    mlp_summed = (
        lax.psum_scatter(grad_in, "fsdp", scatter_dimension=0, tiled=True),
        lax.psum_scatter(grad_out, "fsdp", scatter_dimension=0, tiled=True),
        lax.psum_scatter(grad_bias_in, "fsdp", scatter_dimension=0, tiled=True),
        lax.psum_scatter(grad_bias_out, "fsdp", scatter_dimension=0, tiled=True),
        lax.psum_scatter(grad_gain_two, "fsdp", scatter_dimension=0, tiled=True),
        lax.psum_scatter(grad_shift_two, "fsdp", scatter_dimension=0, tiled=True),
    )
    grad_attn = grad_h.astype(half)
    grad_bias_output = column_sums(grad_attn)
    grad_output = jnp.dot(regathered.T, grad_attn, preferred_element_type=single)
    grad_regathered = jnp.dot(grad_attn, full_output.T, preferred_element_type=single).astype(half)
    grad_mixed = lax.all_to_all(grad_regathered, "seq", split_axis=1, concat_axis=0, tiled=True)
    grad_mixed_blocks = grad_mixed.reshape(block_count, block_rows, heads_here, HD)

    def backward_block(grad_carry, block_parts):
        grad_keys, grad_values = grad_carry
        query_block, block_total, grad_block = block_parts
        scores = (
            jnp.einsum("qhd,khd->hqk", query_block, key_heads, preferred_element_type=single)
            * 0.125
        )
        attn_probs = jnp.exp(scores - block_total[..., None])
        grad_probs = jnp.einsum(
            "qhd,khd->hqk", grad_block, value_heads, preferred_element_type=single
        )
        row_delta = jnp.sum(attn_probs * grad_probs, axis=-1, keepdims=True)
        grad_scores = (attn_probs * (grad_probs - row_delta)).astype(half)
        grad_query = (
            jnp.einsum("hqk,khd->qhd", grad_scores, key_heads, preferred_element_type=single)
            * 0.125
        )
        grad_keys = (
            grad_keys
            + jnp.einsum("hqk,qhd->khd", grad_scores, query_block, preferred_element_type=single)
            * 0.125
        )
        grad_values = grad_values + jnp.einsum(
            "hqk,qhd->khd", attn_probs.astype(half), grad_block, preferred_element_type=single
        )
        return ((grad_keys, grad_values), grad_query.astype(half))

    zero_grads = jnp.zeros((seq_length, heads_here, HD), single)
    (grad_keys, grad_values), grad_query_blocks = lax.scan(
        backward_block, (zero_grads, zero_grads), (query_blocks, log_total, grad_mixed_blocks)
    )
    grad_heads = jnp.stack(
        [
            grad_query_blocks.reshape(seq_length, local_width),
            grad_keys.reshape(seq_length, local_width).astype(half),
            grad_values.reshape(seq_length, local_width).astype(half),
        ]
    )
    grad_tokens = lax.all_to_all(grad_heads, "seq", split_axis=1, concat_axis=2, tiled=True)
    grad_query_rows = grad_tokens[0]
    grad_key_rows = grad_tokens[1]
    grad_value_rows = grad_tokens[2]
    grad_query = jnp.dot(tokens.T, grad_query_rows, preferred_element_type=single)
    grad_key = jnp.dot(tokens.T, grad_key_rows, preferred_element_type=single)
    grad_value = jnp.dot(tokens.T, grad_value_rows, preferred_element_type=single)
    grad_bias_query = column_sums(grad_query_rows)
    grad_bias_value = column_sums(grad_value_rows)
    input_grad = grad_h + jnp.dot(grad_query_rows, full_query.T, preferred_element_type=single)
    input_grad = input_grad + jnp.dot(grad_key_rows, full_key.T, preferred_element_type=single)
    input_grad = input_grad + jnp.dot(grad_value_rows, full_value.T, preferred_element_type=single)
    attn_summed = (
        lax.psum_scatter(grad_query, "fsdp", scatter_dimension=0, tiled=True),
        lax.psum_scatter(grad_key, "fsdp", scatter_dimension=0, tiled=True),
        lax.psum_scatter(grad_value, "fsdp", scatter_dimension=0, tiled=True),
        lax.psum_scatter(grad_output, "fsdp", scatter_dimension=0, tiled=True),
        lax.psum_scatter(grad_bias_query, "fsdp", scatter_dimension=0, tiled=True),
        lax.psum_scatter(grad_bias_value, "fsdp", scatter_dimension=0, tiled=True),
        lax.psum_scatter(grad_bias_output, "fsdp", scatter_dimension=0, tiled=True),
        lax.psum_scatter(grad_gain_one, "fsdp", scatter_dimension=0, tiled=True),
        lax.psum_scatter(grad_shift_one, "fsdp", scatter_dimension=0, tiled=True),
    )
    summed = lax.psum(
        (
            attn_summed[0],
            attn_summed[1],
            attn_summed[2],
            attn_summed[3],
            attn_summed[4],
            attn_summed[5],
            attn_summed[6],
            attn_summed[7],
            attn_summed[8],
            mlp_summed[0],
            mlp_summed[1],
            mlp_summed[2],
            mlp_summed[3],
            mlp_summed[4],
            mlp_summed[5],
        ),
        "seq",
    )
    results = (
        summed[0],
        summed[1],
        summed[2],
        summed[3],
        summed[4],
        summed[5],
        summed[6],
        summed[7],
        summed[8],
        summed[9],
        summed[11],
        summed[10],
        summed[12],
        summed[13],
        summed[14],
    )
    return (
        layer_out.astype(half).reshape(layer_input.shape),
        input_grad.reshape(layer_input.shape),
        results[0],
        results[1],
        results[2],
        results[3],
        results[4],
        results[5],
        results[6],
        results[7],
        results[8],
        results[9],
        results[10],
        results[11],
        results[12],
        results[13],
        results[14],
        rms_values,
    )


def solution(mesh):
    placed = (
        P("fsdp", "seq", None),
        P("fsdp", None),
        P("fsdp", None),
        P("fsdp", None),
        P("fsdp", None),
        P("fsdp"),
        P("fsdp"),
        P("fsdp"),
        P("fsdp"),
        P("fsdp"),
        P("fsdp", None),
        P("fsdp"),
        P("fsdp", None),
        P("fsdp"),
        P("fsdp"),
        P("fsdp"),
        P("fsdp", "seq", None),
    )
    return jax.shard_map(
        local,
        mesh=mesh,
        in_specs=placed,
        out_specs=(
            P("fsdp", "seq", None),
            P("fsdp", "seq", None),
            P("fsdp", None),
            P("fsdp", None),
            P("fsdp", None),
            P("fsdp", None),
            P("fsdp"),
            P("fsdp"),
            P("fsdp"),
            P("fsdp"),
            P("fsdp"),
            P("fsdp", None),
            P("fsdp"),
            P("fsdp", None),
            P("fsdp"),
            P("fsdp"),
            P("fsdp"),
            P(),
        ),
        check_vma=False,
    )
```

profile of v0, /device:TPU:25, one launch (start us, length us, event | category | flops | bytes accessed | tf_op | source)
XLA Modules:
  0.0 1653.1 jit_solution(8044954652545755404)
XLA Ops:
  10.6 12.7 all-gather
  23.3 14.0 all-gather.1
  37.3 21.6 %all-gather.18.cloned.1.call-done = bf16[1024,1024]{1,0:T(8,128)(2,1)} async-done(((bf16[128,1024]{1,0:T(8,128)(2,1)}), bf16[1024,1024]{1,0:T(8,128)(2,1)}) %all-gather.18.cloned.1.call-update) | async-done | bytes 2097168 | tf_op jit(solution)/shard_map/all_gather | solution.py:58
  61.7 47.1 %all-gather.16.cloned.1.call-done = bf16[1024,1024]{1,0:T(8,128)(2,1)} async-done(((bf16[128,1024]{1,0:T(8,128)(2,1)}), bf16[1024,1024]{1,0:T(8,128)(2,1)}) %all-gather.16.cloned.1.call-update) | async-done | bytes 2097168 | tf_op jit(solution)/shard_map/all_gather | solution.py:57
  112.3 46.5 %all-gather.20.cloned.1.call-done = bf16[1024,1024]{1,0:T(8,128)(2,1)} async-done(((bf16[128,1024]{1,0:T(8,128)(2,1)}), bf16[1024,1024]{1,0:T(8,128)(2,1)}) %all-gather.20.cloned.1.call-update) | async-done | bytes 2097168 | tf_op jit(solution)/shard_map/all_gather | solution.py:59
  170.5 35.6 %all-to-all-done = bf16[3,384,1024]{1,0,2:T(4,128)(2,1)S(1)} async-done(((bf16[3,384,1024]{1,0,2:T(4,128)(2,1)}), bf16[3,384,1024]{1,0,2:T(4,128)(2,1)S(1)}, u32[]{:S(2)}, u32[]{:S(2)}) %all-to-all-start) | async-done | bytes 2359328 | tf_op jit(solution)/shard_map/all_to_all | solution.py:87
  215.3 25.2 %while.27 = (s32[]{:T(128)}, bf16[3,512,4,64]{1,3,2,0:T(8,128)(2,1)}, f32[3,4,512]{2,1,0:T(4,128)S(1)}, bf16[3,512,4,64]{1,3,2,0:T(8,128)(2,1)S(1)}, bf16[1536,4...) while((s32[]{:T(128)}, bf16[3,512,4,64]{1,3,2,0:T(8,128)(2,1)}, ...), condition=%wide.region_3.4_spmd, body=%wide.region_0.3_spmd.sunk | while | flops 833746944 | bytes 39912020 | solution.py:112
  248.9 4.9 all-to-all-start.1
  253.8 11.6 all-gather.2
  265.5 15.7 all-gather.3
  281.1 13.0 all-gather.4
  294.2 22.6 %all-gather.5 = bf16[8,1,512]{2,1,0:T(2,128)(2,1)S(1)} all-gather(bf16[1,1,512]{2,1,0:T(2,128)(2,1)S(1)} %reshape.201), channel_id=1, replica_groups=mesh['seq'=4,'fsdp'=8] {'fsdp'}, dimensions={0}, use_global_device_ids=true | all-gather | bytes 9216 | tf_op jit(solution)/shard_map/all_gather | solution.py:70
  316.9 13.9 all-gather.6
  330.7 13.2 all-gather.7
  344.0 14.3 all-gather.8
  363.7 21.0 %multiply_convert_fusion.1 = (bf16[384,4096]{1,0:T(8,128)(2,1)}, f32[384,4096]{1,0:T(8,128)}, f32[384,4096]{1,0:T(8,128)}) fusion(f32[4096]{0:T(1024)S(1)} %bitcast.246, bf16[1024,4096]{1,0:T(8,128)(2,1)} %all-gather.24.cloned.1.call-done, f32[384,1024]{1,0:T(8,128)} %copy-done.7, f32[1024]{0:T(1024)S(1)} %bitcast.235, f32[1024]{0:T(1024)S(1)} %bitcast.230, ...), kind=kOutput, calls=%fused_computation.50 | convolution fusion | flops 3327000576 | bytes 25717760 | tf_op jit(solution)/shard_map/dot_general | solution.py:122
  384.7 74.8 %all-gather.26.cloned.1.call-done = bf16[4096,1024]{1,0:T(8,128)(2,1)} async-done(((bf16[512,1024]{1,0:T(8,128)(2,1)}), bf16[4096,1024]{1,0:T(8,128)(2,1)}) %all-gather.26.cloned.1.call-update) | async-done | bytes 8388624 | tf_op jit(solution)/shard_map/all_gather | solution.py:69
  459.5 9.0 fusion.73
  472.6 14.0 convert_reduce_fusion
  498.8 4.6 all-to-all-start.2
  503.4 4.7 fusion.80
  508.2 6.1 all-to-all-done.2
  524.0 84.8 %while.28 = (s32[]{:T(128)}, f32[1536,4,64]{0,2,1:T(8,128)}, f32[1536,4,64]{0,2,1:T(8,128)}, bf16[3,512,4,64]{1,3,2,0:T(8,128)(2,1)}, bf16[3,512,4,64]{1,3,2,0:T...) while((s32[]{:T(128)}, f32[1536,4,64]{0,2,1:T(8,128)}, ...), condition=%wide.region_14.15_spmd.clone, body=%wide.region_12.14_spmd.clone.sunk | while | flops 2053240832 | bytes 211347216 | solution.py:196
  525.9 4.9 multiply_reduce_fusion.13
  530.8 4.6 multiply_convert_fusion.3
  535.4 5.3 fusion.148
  540.7 6.4 fusion.150
  547.0 4.7 fusion.149
  553.6 4.9 multiply_reduce_fusion.13
  563.1 5.8 fusion.148
  568.8 6.2 fusion.150
  575.1 5.2 fusion.149
  582.2 4.9 multiply_reduce_fusion.13
  591.6 5.8 fusion.148
  597.4 6.2 fusion.150
  603.6 5.2 fusion.149
  619.4 39.7 %all_to_all.65 = bf16[3,1536,256]{2,0,1:T(4,128)(2,1)S(1)} all-to-all(bf16[3,1536,256]{2,0,1:T(4,128)(2,1)S(1)} %copy.76), channel_id=1, replica_groups=mesh['seq'=4,'fsdp'=8] {'seq'}, dimensions={1} | all-to-all | bytes 4718592 | tf_op jit(solution)/shard_map/all_to_all | solution.py:206
  681.5 13.1 fusion.68
  694.9 12.5 fusion.81
  707.4 46.5 %reduce-scatter.11.cloned.1.call-done = f32[128,1024]{0,1:T(8,128)} async-done(((f32[1024,1024]{0,1:T(8,128)}), f32[128,1024]{0,1:T(8,128)}) %reduce-scatter.11.cloned.1.call-update) | async-done | bytes 524304 | tf_op jit(solution)/shard_map/reduce_scatter | solution.py:221
  753.9 91.7 %reduce-scatter.7.cloned.1.call-done = f32[128,1024]{0,1:T(8,128)} async-done(((f32[1024,1024]{0,1:T(8,128)}), f32[128,1024]{0,1:T(8,128)}) %reduce-scatter.7.cloned.1.call-update) | async-done | bytes 524304 | tf_op jit(solution)/shard_map/reduce_scatter | solution.py:219
  845.6 92.1 %reduce-scatter.9.cloned.1.call-done = f32[128,1024]{0,1:T(8,128)} async-done(((f32[1024,1024]{0,1:T(8,128)}), f32[128,1024]{0,1:T(8,128)}) %reduce-scatter.9.cloned.1.call-update) | async-done | bytes 524304 | tf_op jit(solution)/shard_map/reduce_scatter | solution.py:220
  937.8 286.0 %reduce-scatter.15.cloned.1.call-done = f32[128,4096]{1,0:T(8,128)} async-done(((f32[1024,4096]{1,0:T(8,128)}), f32[128,4096]{1,0:T(8,128)}) %reduce-scatter.15.cloned.1.call-update) | async-done | bytes 2097168 | tf_op jit(solution)/shard_map/reduce_scatter | solution.py:154
  1223.8 285.9 %reduce-scatter.17.cloned.1.call-done = f32[512,1024]{1,0:T(8,128)} async-done(((f32[4096,1024]{1,0:T(8,128)}), f32[512,1024]{1,0:T(8,128)}) %reduce-scatter.17.cloned.1.call-update) | async-done | bytes 2097168 | tf_op jit(solution)/shard_map/reduce_scatter | solution.py:155
  1516.8 40.3 %psum.127 = f32[5]{0:T(128)S(1)} all-reduce(f32[5]{0:T(128)S(1)} %stack.45), channel_id=1, replica_groups=mesh['seq'=4,'fsdp'=8] {'seq','fsdp'}, use_global_device_ids=true, to_apply=%region_59.60 | all-reduce | flops 5 | bytes 40 | tf_op jit(solution)/shard_map/psum | solution.py:140
  1558.0 27.2 %all-reduce.9 = (f32[1024]{0:T(1024)S(1)}, f32[1024]{0:T(1024)S(1)}, f32[1024]{0:T(1024)S(1)}, f32[1024]{0:T(1024)S(1)}, f32[1024]{0:T(1024)S(1)}, /*index=5*/f3...) all-reduce(f32[1024]{0:T(1024)S(1)} %bitcast.244, ...), channel_id=6, replica_groups=mesh['seq'=4,'fsdp'=8] {'fsdp'}, use_global_device_ids=true, to_apply=%region_24.25.clone | all-reduce | flops 12288 | bytes 98304
  1585.8 14.6 all-reduce.10
  1608.1 26.7 %all-reduce.14.cloned.1.call-done = (f32[128,1024]{0,1:T(8,128)}, f32[128,1024]{0,1:T(8,128)}, f32[128,1024]{0,1:T(8,128)}, f32[128,1024]{1,0:T(8,128)}, f32[128,4096]{1,0:T(8,128)}, /*index=5*/f32[512,1024]{1,0:T(8,128)}) async-done(((f32[128,1024]{0,1:T(8,128)}, f32[128,1024]{0,1:T(8,128)}, f32[128,1024]{0,1:T(8,128)}, f32[128,1024]{1,0:T(8,128)}, f32[128,4096]{1,0:T(8,128)}, ...) | async-done | bytes 6291472 | tf_op jit(solution)/shard_map/psum | solution.py:229
  (252 shorter events, 169.7 us)
Async XLA Ops:
  7.2 51.7 %all-gather.18.cloned.1.call-start = ((), (), s32[]{:S(2)}) async-start(), calls=%async_computation.11 | async-start | bytes 2359296 | tf_op jit(solution)/shard_map/all_gather | solution.py:58
  7.9 100.9 %all-gather.16.cloned.1.call-start = ((), (), s32[]{:S(2)}) async-start(), calls=%async_computation.10 | async-start | bytes 2359296 | tf_op jit(solution)/shard_map/all_gather | solution.py:57
  8.7 150.1 %all-gather.20.cloned.1.call-start = ((), (), s32[]{:S(2)}) async-start(), calls=%async_computation.12 | async-start | bytes 2359296 | tf_op jit(solution)/shard_map/all_gather | solution.py:59
  9.4 348.9 %all-gather.22.cloned.1.call-start = ((), (), s32[]{:S(2)}) async-start(), calls=%async_computation.13 | async-start | bytes 2359296 | tf_op jit(solution)/shard_map/all_gather | solution.py:60
  10.0 98.8 %copy-start.10 = (bf16[1,384,1024]{2,1,0:T(8,128)(2,1)S(1)}, bf16[1,384,1024]{2,1,0:T(8,128)(2,1)}, u32[]{:S(2)}) copy-start(bf16[1,384,1024]{2,1,0:T(8,128)(2,1)} %param.21) | copy-start | bytes 2359300
  10.0 353.7 %all-gather.24.cloned.1.call-start = ((), (), s32[]{:S(2)}) async-start(), calls=%async_computation.14 | async-start | bytes 9437184 | tf_op jit(solution)/shard_map/all_gather | solution.py:68
  165.5 40.6 %all-to-all-start = ((bf16[3,384,1024]{1,0,2:T(4,128)(2,1)}), bf16[3,384,1024]{1,0,2:T(4,128)(2,1)S(1)}, u32[]{:S(2)}, u32[]{:S(2)}) async-start(bf16[3,384,1024]{1,0,2:T(4,128)(2,1)} %copy.66), calls=%async_computation | async-start | bytes 6291456 | tf_op jit(solution)/shard_map/all_to_all | solution.py:87
  169.9 289.6 %all-gather.26.cloned.1.call-start = ((), (), s32[]{:S(2)}) async-start(), calls=%async_computation.15 | async-start | bytes 9437184 | tf_op jit(solution)/shard_map/all_gather | solution.py:69
  240.5 13.4 copy-start.36
  240.5 25.0 %copy-start.37 = (bf16[128]{0:T(256)(128)(2,1)S(1)}, bf16[128]{0:T(256)(128)(2,1)}, u32[]{:S(2)}) copy-start(bf16[128]{0:T(256)(128)(2,1)} %param.29) | copy-start | bytes 772
  240.5 40.7 %copy-start.38 = (bf16[128]{0:T(256)(128)(2,1)S(1)}, bf16[128]{0:T(256)(128)(2,1)}, u32[]{:S(2)}) copy-start(bf16[128]{0:T(256)(128)(2,1)} %param.30) | copy-start | bytes 772
  240.5 53.7 %copy-start.35 = (bf16[512]{0:T(512)(128)(2,1)S(1)}, bf16[512]{0:T(512)(128)(2,1)}, u32[]{:S(2)}) copy-start(bf16[512]{0:T(512)(128)(2,1)} %param.32) | copy-start | bytes 3076
  240.5 76.4 %copy-start.39 = (bf16[128]{0:T(256)(128)(2,1)S(1)}, bf16[128]{0:T(256)(128)(2,1)}, u32[]{:S(2)}) copy-start(bf16[128]{0:T(256)(128)(2,1)} %param.34) | copy-start | bytes 772
  240.5 90.2 %copy-start.40 = (bf16[128]{0:T(256)(128)(2,1)S(1)}, bf16[128]{0:T(256)(128)(2,1)}, u32[]{:S(2)}) copy-start(bf16[128]{0:T(256)(128)(2,1)} %param.35) | copy-start | bytes 772
  240.5 103.5 %copy-start.41 = (bf16[128]{0:T(256)(128)(2,1)S(1)}, bf16[128]{0:T(256)(128)(2,1)}, u32[]{:S(2)}) copy-start(bf16[128]{0:T(256)(128)(2,1)} %param.36) | copy-start | bytes 772
  248.9 109.4 %all-to-all-start.1 = ((bf16[4,384,256]{1,2,0:T(8,128)(2,1)}), bf16[4,384,256]{1,2,0:T(8,128)(2,1)}, u32[]{:S(2)}, u32[]{:S(2)}) async-start(bf16[4,384,256]{1,2,0:T(8,128)(2,1)} %copy.70), calls=%async_computation.1 | async-start | bytes 1572864 | tf_op jit(solution)/shard_map/all_to_all | solution.py:114
  281.1 210.0 %copy-start.19 = (f32[8,1,128]{2,1,0:T(1,128)}, f32[8,1,128]{2,1,0:T(1,128)S(1)}, u32[]{:S(2)}) copy-start(f32[8,1,128]{2,1,0:T(1,128)S(1)} %convert_element_type.164) | copy-start | bytes 12292
  294.2 192.4 %copy-start.21 = (f32[8,1,128]{2,1,0:T(1,128)}, f32[8,1,128]{2,1,0:T(1,128)S(1)}, u32[]{:S(2)}) copy-start(f32[8,1,128]{2,1,0:T(1,128)S(1)} %convert_element_type.165) | copy-start | bytes 12292
  362.2 128.9 %copy-start.23 = (f32[384]{0:T(512)}, f32[384]{0:T(512)S(1)}, u32[]{:S(2)}) copy-start(f32[384]{0:T(512)S(1)} %broadcast_multiply_fusion.1) | copy-start | bytes 4612
  363.7 127.4 %copy-start.25 = (f32[384]{0:T(512)}, f32[384]{0:T(512)S(1)}, u32[]{:S(2)}) copy-start(f32[384]{0:T(512)S(1)} %fusion.66) | copy-start | bytes 4612
  459.5 9.3 copy-start.9
  471.2 15.4 slice-start
  472.5 14.0 copy-start.12
  472.5 14.0 copy-start.8
  472.6 14.0 slice-start.1
  498.8 15.5 all-to-all-start.2
  503.4 204.0 %reduce-scatter.13.cloned.1.call-start = ((), (), s32[]{:S(2)}) async-start(), calls=%async_computation.19 | async-start | bytes 4718592 | tf_op jit(solution)/shard_map/reduce_scatter | solution.py:222
  508.1 245.8 %reduce-scatter.11.cloned.1.call-start = ((), (), s32[]{:S(2)}) async-start(), calls=%async_computation.18 | async-start | bytes 4718592 | tf_op jit(solution)/shard_map/reduce_scatter | solution.py:221
  525.8 4.9 copy-start
  535.4 11.7 copy-start.1
  563.1 12.0 copy-start.1
  575.1 5.2 copy-start.4
  582.1 4.9 copy-start
  591.6 12.0 copy-start.1
  603.6 5.2 copy-start.4
  666.8 178.9 %reduce-scatter.7.cloned.1.call-start = ((), (), s32[]{:S(2)}) async-start(), calls=%async_computation.16 | async-start | bytes 4718592 | tf_op jit(solution)/shard_map/reduce_scatter | solution.py:219
  673.7 264.1 %reduce-scatter.9.cloned.1.call-start = ((), (), s32[]{:S(2)}) async-start(), calls=%async_computation.17 | async-start | bytes 4718592 | tf_op jit(solution)/shard_map/reduce_scatter | solution.py:220
  680.8 543.0 %reduce-scatter.15.cloned.1.call-start = ((), (), s32[]{:S(2)}) async-start(), calls=%async_computation.20 | async-start | bytes 18874368 | tf_op jit(solution)/shard_map/reduce_scatter | solution.py:154
  694.6 815.1 %reduce-scatter.17.cloned.1.call-start = ((), (), s32[]{:S(2)}) async-start(), calls=%async_computation.21 | async-start | bytes 18874368 | tf_op jit(solution)/shard_map/reduce_scatter | solution.py:155
  707.4 927.5 %all-reduce.14.cloned.1.call-start = ((), (), s32[]{:S(2)}) async-start(), calls=%async_computation.22 | async-start | bytes 12582912 | tf_op jit(solution)/shard_map/psum | solution.py:229
  1509.7 48.2 %copy-start.29 = (f32[1024]{0:T(1024)S(1)}, f32[1024]{0:T(1024)}, u32[]{:S(2)}) copy-start(f32[1024]{0:T(1024)} %get-tuple-element.254) | copy-start | bytes 12292
  1509.7 48.2 %copy-start.30 = (f32[1024]{0:T(1024)S(1)}, f32[1024]{0:T(1024)}, u32[]{:S(2)}) copy-start(f32[1024]{0:T(1024)} %get-tuple-element.315) | copy-start | bytes 12292
  1509.7 48.2 %copy-start.31 = (f32[1024]{0:T(1024)S(1)}, f32[1024]{0:T(1024)}, u32[]{:S(2)}) copy-start(f32[1024]{0:T(1024)} %get-tuple-element.319) | copy-start | bytes 12292
  1509.7 48.2 %copy-start.32 = (f32[4096]{0:T(1024)S(1)}, f32[4096]{0:T(1024)}, u32[]{:S(2)}) copy-start(f32[4096]{0:T(1024)} %get-tuple-element.317) | copy-start | bytes 49156
  1509.7 48.2 %copy-start.33 = (f32[1024]{0:T(1024)S(1)}, f32[1024]{0:T(1024)}, u32[]{:S(2)}) copy-start(f32[1024]{0:T(1024)} %get-tuple-element.252) | copy-start | bytes 12292
  1509.7 48.2 %copy-start.34 = (f32[1024]{0:T(1024)S(1)}, f32[1024]{0:T(1024)}, u32[]{:S(2)}) copy-start(f32[1024]{0:T(1024)} %get-tuple-element.260) | copy-start | bytes 12292
  1634.8 6.3 copy-start.18
  1638.9 6.1 copy-start.16
  (23 other events, 51.8 us)
Sparse Core Ops, SparseCore 0:
  10.1 48.7 all-gather.17
  61.0 47.7 all-gather.15
  111.0 47.7 all-gather.19
  160.7 47.7 all-gather.21
  210.5 123.5 all-gather.23
  336.1 123.3 all-gather.25
  508.2 86.8 reduce-scatter.12
  666.9 86.9 reduce-scatter.10
  757.5 88.0 reduce-scatter.6
  849.6 88.1 reduce-scatter.8
  941.6 282.2 reduce-scatter.14
  1227.9 281.7 reduce-scatter.16
  1512.5 122.2 all-reduce.13
where the time goes:
time: 1660 us; the launch traced here: 1650 us
  waiting for transfers between devices  1060 us (64%)
  blocking collectives  253 us (15%)
  matrix products  203 us (12%)
  local copies, waits for them, and re-layouts  70.4 us (4%)
  other arithmetic  31.7 us (2%)
    reduce_scatter x1, waiting for transfers between devices, local(): lax.psum_scatter(grad_in, 'fsdp', scatter_dimension=0, tiled=True)  286 us
    reduce_scatter x1, waiting for transfers between devices, local(): lax.psum_scatter(grad_out, 'fsdp', scatter_dimension=0, tiled=True)  286 us
    reduce_scatter x1, waiting for transfers between devices, local(): lax.psum_scatter(grad_key, 'fsdp', scatter_dimension=0, tiled=True)  92.1 us
    reduce_scatter x1, waiting for transfers between devices, local(): lax.psum_scatter(grad_query, 'fsdp', scatter_dimension=0, tiled=True)  91.7 us
    all_gather x1, waiting for transfers between devices, local(): lax.all_gather(out_weight, 'fsdp', axis=0, tiled=True)  74.8 us
    all_gather x1, waiting for transfers between devices, local(): lax.all_gather(query_weight, 'fsdp', axis=0, tiled=True)  47.1 us
    all_gather x1, waiting for transfers between devices, local(): lax.all_gather(value_weight, 'fsdp', axis=0, tiled=True)  46.5 us
    reduce_scatter x1, waiting for transfers between devices, local(): lax.psum_scatter(grad_value, 'fsdp', scatter_dimension=0, tiled=True)  46.5 us
  transfers between devices with their start and end apart: 16, of which 12 were waited for; matrix products, arithmetic and copies ran while one was open for 15% of the time, Pallas kernels for 0%

commit v1 on v0

v1 whole, which is shorter than its diff:
```python
import functools
import jax
import jax.numpy as jnp
from jax import lax
from jax.experimental import pallas as pl
from jax.experimental.pallas import tpu as pltpu
from jax.sharding import PartitionSpec as P

HD = 64
MESH = pl.DeviceIdType.MESH
bf16 = jnp.bfloat16
f32 = jnp.float32


def each(lo, hi, body):
    if hi - lo <= 8:
        for i in range(lo, hi):
            body(i)
    else:
        pl.loop(lo, hi)(body)


class Grid:
    def __init__(self, seq_count, fsdp_count):
        self.S, self.F = seq_count, fsdp_count
        self.H = seq_count // 2
        self.Y = 2 if fsdp_count % 2 == 0 and fsdp_count <= 8 else 4
        self.Z = fsdp_count // self.Y
        self.s = lax.axis_index("seq")
        self.f = lax.axis_index("fsdp")
        self.c = self.s % 2
        self.hi = self.s // 2
        self.z = self.f // self.Y
        self.y = self.f % self.Y

    def zp(self, k):
        return ((self.z + k) % self.Z) * self.Y + self.y

    def yp(self, j):
        return self.z * self.Y + (self.y + j) % self.Y

    def xp(self, m):
        return ((self.hi + m) % self.H) * 2 + self.c

    def sib(self):
        return self.hi * 2 + 1 - self.c

    def origin(self, r):
        j, k = r // self.Z, r % self.Z
        return ((self.z + self.Z - k) % self.Z) * self.Y + (self.y + self.Y - j) % self.Y

    def greet(self, barrier):
        count = 0
        for m in range(self.H):
            for flip in range(2):
                if m or flip:
                    to = ((self.hi + m) % self.H) * 2 + (self.c + flip) % 2
                    pl.semaphore_signal(barrier, inc=1, device_id=(to, self.f), device_id_type=MESH)
                    count += 1
        for k in range(1, self.Z):
            pl.semaphore_signal(barrier, inc=1, device_id=(self.s, self.zp(k)), device_id_type=MESH)
            count += 1
        for j in range(1, self.Y):
            pl.semaphore_signal(barrier, inc=1, device_id=(self.s, self.yp(j)), device_id_type=MESH)
            count += 1
        pl.semaphore_wait(barrier, count)


class Sems:
    def __init__(self):
        self.n = 0

    def take(self, n):
        at = self.n
        self.n += n
        return at


def rcopy(sems, src, dst, send, recv, to):
    return pltpu.make_async_remote_copy(
        src_ref=src,
        dst_ref=dst,
        send_sem=sems.at[send],
        recv_sem=sems.at[recv],
        device_id=to,
        device_id_type=MESH,
    )


class Gather:
    def __init__(self, alloc, S, F, Y, kind):
        self.kind = kind
        Z = F // Y
        self.zs = alloc.take(Z)
        self.ys = alloc.take(Y * Z)
        self.ir = alloc.take(F)
        if kind != "own":
            self.ss, self.sr = alloc.take(F), alloc.take(F)
        if kind == "quarter":
            H = S // 2
            self.xs, self.xr = alloc.take(H * F), alloc.take(H * F)
            self.ts, self.tr = alloc.take(H * F), alloc.take(H * F)

    def bind(self, g, sems, piece, place):
        self.g, self.sems, self.piece, self.place = g, sems, piece, place

    def part(self, hi=None, c=None):
        g = self.g
        c = g.c if c is None else c
        hi = g.hi if hi is None else hi
        return {"own": g.s, "half": c, "quarter": hi * 2 + c}[self.kind]

    def start(self):
        g, p = self.g, self.part()
        src, dst = self.piece(p), self.place(g.f, p)
        for k in range(1, g.Z):
            rcopy(self.sems, src, dst, self.zs + k, self.ir + k, (g.s, g.zp(k))).start()
        for j in range(1, g.Y):
            rcopy(self.sems, src, dst, self.ys + j * g.Z, self.ir + j * g.Z, (g.s, g.yp(j))).start()

    def wait_in(self, r):
        ref = self.place(self.g.origin(r), self.part())
        rcopy(self.sems, ref, ref, self.ir + r, self.ir + r, (self.g.sib(), self.g.f)).wait_recv()

    def pass_on(self, r):
        g = self.g
        ref = self.place(g.origin(r), self.part())
        if self.kind == "quarter":
            for m in range(1, g.H):
                rcopy(self.sems, ref, ref, self.xs + m * g.F + r, self.xr + m * g.F + r, (g.xp(m), g.f)).start()
        if self.kind != "own":
            rcopy(self.sems, ref, ref, self.ss + r, self.sr + r, (g.sib(), g.f)).start()

    def on_z(self):
        g = self.g

        def body(k):
            self.wait_in(k)
            ref = self.place(g.origin(k), self.part())
            for j in range(1, g.Y):
                at = j * g.Z + k
                rcopy(self.sems, ref, ref, self.ys + at, self.ir + at, (g.s, g.yp(j))).start()
            self.pass_on(k)

        each(1, g.Z, body)

    def on_y(self):
        def body(r):
            self.wait_in(r)
            self.pass_on(r)

        each(self.g.Z, self.g.F, body)

    def on_x(self):
        if self.kind != "quarter":
            return
        g = self.g
        for m in range(1, g.H):
            part = self.part(hi=(g.hi + g.H - m) % g.H)

            def body(r):
                ref = self.place(g.origin(r), part)
                at = m * g.F + r
                rcopy(self.sems, ref, ref, self.xr + at, self.xr + at, (g.sib(), g.f)).wait_recv()
                rcopy(self.sems, ref, ref, self.ts + at, self.tr + at, (g.sib(), g.f)).start()

            each(1, g.F, body)

    def finish(self):
        g = self.g
        other = 1 - g.c

        def sent(ref, at):
            rcopy(self.sems, ref, ref, at, at, (g.sib(), g.f)).wait_send()

        def got(ref, at):
            rcopy(self.sems, ref, ref, at, at, (g.sib(), g.f)).wait_recv()

        if self.kind != "own":
            each(1, g.F, lambda r: got(self.place(g.origin(r), self.part(c=other)), self.sr + r))
        if self.kind == "quarter":
            for m in range(1, g.H):
                part = self.part(hi=(g.hi + g.H - m) % g.H, c=other)
                each(1, g.F, lambda r: got(self.place(g.origin(r), part), self.tr + m * g.F + r))
        mine = self.piece(self.part())
        for k in range(1, g.Z):
            sent(mine, self.zs + k)
        for j in range(1, g.Y):
            each(0, g.Z, lambda k: sent(mine, self.ys + j * g.Z + k))
        if self.kind != "own":
            each(1, g.F, lambda r: sent(mine, self.ss + r))
        if self.kind == "quarter":
            for m in range(1, g.H):
                each(1, g.F, lambda r: sent(mine, self.xs + m * g.F + r))
                each(1, g.F, lambda r: sent(mine, self.ts + m * g.F + r))


def forward_kernel(plan, x, wq, wk, wv, small, wo, w1, w2, *rest):
    (xfull, wqkv, smalls, q_o, k_o, v_o, qt_o, kt_o, ot_o, lse_o, mixed, wo_f, w1_f, w2_f) = rest[:14]
    (xs, ws, sm, qn, kn, vn, qt, kt, vt, ot, lse, oblk, onat, sems) = rest[14:]
    S, F, rows, length, heads, wide, vec = plan.S, plan.F, plan.rows, plan.length, plan.heads, plan.wide, plan.vec
    g = Grid(S, F)
    g.greet(pltpu.get_barrier_semaphore())
    part_rows = wq.shape[0]
    local = []

    def keep(src, dst, at):
        copy = pltpu.make_async_copy(src, dst, sems.at[at])
        copy.start()
        return copy

    mine = xs.at[pl.ds(g.s * rows, rows)]
    x_out = [rcopy(sems, x, mine, plan.x_s, plan.x_r, (g.sib(), g.f))]
    for m in range(1, g.H):
        x_out.append(rcopy(sems, x, mine, plan.x_s + m, plan.x_r + m, (g.xp(m), g.f)))
    for copy in x_out[::-1]:
        copy.start()
    for item, src, col in ((plan.gq, wq, 0), (plan.gk, wk, 1), (plan.gv, wv, 2)):
        item.bind(
            g,
            sems,
            lambda p, src=src: src.at[:, pl.ds(p * wide, wide)],
            lambda o, p, col=col: ws.at[pl.ds(o * part_rows, part_rows), pl.ds(col * wide, wide)],
        )
        item.start()
    plan.gs.bind(g, sems, lambda p: small, lambda o, p: sm.at[pl.ds(o * 16, 16)])
    plan.gs.start()
    local.append(keep(x, mine, plan.l))
    for col, src in enumerate((wq, wk, wv)):
        local.append(
            keep(
                src.at[:, pl.ds(g.s * wide, wide)],
                ws.at[pl.ds(g.f * part_rows, part_rows), pl.ds(col * wide, wide)],
                plan.l + 1 + col,
            )
        )
    local.append(keep(small, sm.at[pl.ds(g.f * 16, 16)], plan.l + 4))
    own = []
    for i, (src, dst) in enumerate(((wo, wo_f), (w1, w1_f), (w2, w2_f))):
        n = src.shape[0]
        own.append(keep(src, dst.at[pl.ds(g.f * n, n)], plan.l + 5 + i))
    for src, dst, (item, lo, width) in [
        (src, dst, entry)
        for src, dst, entries in ((wo, wo_f, plan.go), (w1, w1_f, plan.g1), (w2, w2_f, plan.g2))
        for entry in entries
    ]:
        n = src.shape[0]
        item.bind(
            g,
            sems,
            lambda p, src=src, lo=lo, width=width: src.at[:, pl.ds(lo + p * width, width)],
            lambda o, p, dst=dst, n=n, lo=lo, width=width: dst.at[pl.ds(o * n, n), pl.ds(lo + p * width, width)],
        )
    big = [e[0] for e in plan.g1 + plan.go + plan.g2]
    for item in (plan.gq, plan.gk, plan.gv, plan.gs):
        item.on_z()
    x_pass = []
    for m in range(1, g.H):
        theirs = xs.at[pl.ds(((g.hi + g.H - m) % g.H * 2 + g.c) * rows, rows)]
        rcopy(sems, theirs, theirs, plan.x_s, plan.x_r + m, (g.sib(), g.f)).wait_recv()
        copy = rcopy(sems, theirs, theirs, plan.x_s + g.H + m, plan.x_r + g.H + m, (g.sib(), g.f))
        copy.start()
        x_pass.append(copy)
    for item in (plan.gq, plan.gk, plan.gv, plan.gs):
        item.on_y()
    for item in big:
        item.start()
    rcopy(sems, mine, mine, plan.x_s, plan.x_r, (g.sib(), g.f)).wait_recv()
    for m in range(1, g.H):
        rcopy(sems, mine, mine, plan.x_s, plan.x_r + g.H + m, (g.sib(), g.f)).wait_recv()
    for copy in local:
        copy.wait()

    table = sm[...]
    lane = lax.broadcasted_iota(jnp.int32, (vec, wide), 1)
    spread = (lane % vec == lax.broadcasted_iota(jnp.int32, (vec, wide), 0)).astype(f32).astype(bf16)
    spread = jnp.dot(table, spread, preferred_element_type=f32)
    row = lax.broadcasted_iota(jnp.int32, spread.shape, 0)
    column = lax.broadcasted_iota(jnp.int32, spread.shape, 1)

    def vector(i):
        want = (g.s * (wide // vec) + column // vec) * 16 + i
        return jnp.sum(jnp.where(row == want, spread, 0.0), axis=0, keepdims=True)

    bias_q, bias_v = vector(0), vector(1)

    @pl.loop(0, S)
    def _(b):
        at = pl.multiple_of(b * rows, rows)
        prod = jnp.dot(xs[pl.ds(at, rows), :], ws[...], preferred_element_type=f32)
        q = (prod[:, :wide] + bias_q).astype(bf16).astype(f32) * 0.125
        k = prod[:, wide : 2 * wide]
        v = prod[:, 2 * wide :] + bias_v
        qn[pl.ds(at, rows), :] = q.astype(bf16)
        kn[pl.ds(at, rows), :] = k.astype(bf16)
        vn[pl.ds(at, rows), :] = v.astype(bf16)
        qt[:, pl.ds(at, rows)] = q.T.astype(bf16)
        kt[:, pl.ds(at, rows)] = k.T.astype(bf16)
        vt[:, pl.ds(at, rows)] = v.T.astype(bf16)

    stores = [
        keep(src, dst, plan.l + 8 + i)
        for i, (src, dst) in enumerate(
            ((xs, xfull), (ws, wqkv), (sm, smalls), (qn, q_o), (kn, k_o), (vn, v_o), (qt, qt_o), (kt, kt_o))
        )
    ]
    head_of = lax.broadcasted_iota(jnp.int32, (wide, rows), 0) // HD
    sent = []
    for t in range(S):
        hi = (g.hi + 1 + t // 2) % g.H
        c = (g.c + t + t // (2 * (g.H - 1))) % 2
        to = hi * 2 + c
        at = pl.multiple_of(to * rows, rows)

        @pl.loop(0, heads)
        def _(h):
            q = jnp.where(head_of == h, qt[:, pl.ds(at, rows)], jnp.zeros((), bf16))
            s = jnp.dot(kn[...], q, preferred_element_type=f32)
            m = jnp.max(s, axis=0, keepdims=True)
            e = jnp.exp(s - m)
            l = jnp.sum(e, axis=0, keepdims=True)
            band = pl.ds(pl.multiple_of(h * HD, HD), HD)
            o = jnp.dot(vt[band, :], e.astype(bf16), preferred_element_type=f32) / l
            oblk[band, :] = o
            lse[pl.ds(h, 1), pl.ds(at, rows)] = m + jnp.log(l)

        ot[:, pl.ds(at, rows)] = oblk[...].astype(bf16)
        onat[t] = oblk[...].T.astype(bf16)
        dst = mixed.at[:, pl.ds(g.s * wide, wide)]
        if t < S - 1:
            copy = rcopy(sems, onat.at[t], dst, plan.o_s + t, plan.o_r + g.s, (to, g.f))
            copy.start()
            sent.append(copy)
        else:
            stores.append(keep(onat.at[t], dst, plan.o_s + t))
    stores.append(keep(ot, ot_o, plan.l + 16))
    stores.append(keep(lse, lse_o, plan.l + 17))
    for i, item in enumerate(big):
        if i == 0:
            item.on_z()
        item.on_y()
        if i + 1 < len(big):
            big[i + 1].on_z()
        item.on_x()
    for item in (plan.gq, plan.gk, plan.gv, plan.gs, *big):
        item.finish()
    for i in range(1, S):
        peer = (g.s + i) % S
        ref = mixed.at[:, pl.ds(peer * wide, wide)]
        rcopy(sems, ref, ref, plan.o_r + peer, plan.o_r + peer, (peer, g.f)).wait_recv()
    for copy in sent + x_out + x_pass:
        copy.wait_send()
    for copy in stores + own:
        copy.wait()


class Plan:
    pass


def forward_plan(S, F, rows, width, ff):
    plan = Plan()
    alloc = Sems()
    plan.S, plan.F, plan.rows, plan.length = S, F, rows, rows * S
    plan.wide = width // S
    plan.heads = plan.wide // HD
    plan.vec = width // F
    Y = 2 if F % 2 == 0 and F <= 8 else 4
    plan.x_s, plan.x_r = alloc.take(S), alloc.take(S)
    plan.gq, plan.gk, plan.gv, plan.gs = (Gather(alloc, S, F, Y, "own") for _ in range(4))
    half = width // 2
    plan.go = [(Gather(alloc, S, F, Y, "half"), 0, half)]
    eighth = ff // 2 // S
    plan.g1 = [(Gather(alloc, S, F, Y, "quarter"), i * S * eighth, eighth) for i in range(2)]
    plan.g2 = [(Gather(alloc, S, F, Y, "half"), i * half, half // 2) for i in range(2)]
    plan.o_s, plan.o_r = alloc.take(S), alloc.take(S)
    plan.l = alloc.take(20)
    plan.sems = alloc.n
    return plan


def forward(S, F, x, wq, wk, wv, small, wo, w1, w2):
    rows, width = x.shape
    ff = w1.shape[1]
    plan = forward_plan(S, F, rows, width, ff)
    length, wide, heads = plan.length, plan.wide, plan.heads
    sds = jax.ShapeDtypeStruct
    any_ = pl.BlockSpec(memory_space=pl.ANY)
    return pl.pallas_call(
        functools.partial(forward_kernel, plan),
        out_shape=(
            sds((length, width), bf16),
            sds((width, 3 * wide), bf16),
            sds((F * 16, plan.vec), bf16),
            sds((length, wide), bf16),
            sds((length, wide), bf16),
            sds((length, wide), bf16),
            sds((wide, length), bf16),
            sds((wide, length), bf16),
            sds((wide, length), bf16),
            sds((8, length), f32),
            sds((rows, width), bf16),
            sds((width, width), bf16),
            sds((width, ff), bf16),
            sds((ff, width), bf16),
        ),
        in_specs=[any_] * 8,
        out_specs=(any_,) * 14,
        scratch_shapes=[
            pltpu.VMEM((length, width), bf16),
            pltpu.VMEM((width, 3 * wide), bf16),
            pltpu.VMEM((F * 16, plan.vec), bf16),
            pltpu.VMEM((length, wide), bf16),
            pltpu.VMEM((length, wide), bf16),
            pltpu.VMEM((length, wide), bf16),
            pltpu.VMEM((wide, length), bf16),
            pltpu.VMEM((wide, length), bf16),
            pltpu.VMEM((wide, length), bf16),
            pltpu.VMEM((wide, length), bf16),
            pltpu.VMEM((8, length), f32),
            pltpu.VMEM((wide, rows), f32),
            pltpu.VMEM((S, rows, wide), bf16),
            pltpu.SemaphoreType.DMA((plan.sems,)),
        ],
        compiler_params=pltpu.CompilerParams(collective_id=0, has_side_effects=True, vmem_limit_bytes=48 << 20),
        name="attention_forward_and_weight_gather",
    )(x, wq, wk, wv, small, wo, w1, w2)


def layer_norm(stream, gain, shift):
    centre = stream - jnp.mean(stream, axis=-1, keepdims=True)
    variance = jnp.mean(centre * centre, axis=-1, keepdims=True)
    return centre * lax.rsqrt(variance + 1e-05) * gain + shift


def gelu_exact(inputs):
    return jax.nn.gelu(inputs, approximate=False)


def column_sums(matrix):
    return jnp.sum(matrix.astype(f32), axis=0)


def local(
    layer_input,
    query_weight,
    key_weight,
    value_weight,
    output_weight,
    query_bias,
    value_bias,
    output_bias,
    attn_gain,
    attn_shift,
    in_weight,
    in_bias,
    out_weight,
    out_bias,
    out_gain,
    out_shift,
    out_cotangent,
):
    F = lax.axis_size("fsdp")
    S = lax.axis_size("seq")
    width = layer_input.shape[-1]
    tokens = layer_input.reshape(-1, width)
    rows = tokens.shape[0]
    vec = query_bias.shape[0]
    vectors = (query_bias, value_bias, output_bias, attn_gain, attn_shift, out_bias, out_gain, out_shift)
    fan = in_bias.shape[0] // vec
    small = jnp.concatenate(
        [v.reshape(1, vec) for v in vectors]
        + [in_bias.reshape(fan, vec), jnp.zeros((16 - len(vectors) - fan, vec), bf16)]
    )
    (xfull, wqkv, smalls, q, k, v, qt, kt, ot, lse, mixed, wo, w1, w2) = forward(
        S, F, tokens, query_weight, key_weight, value_weight, small, output_weight, in_weight, out_weight
    )
    smalls = smalls.reshape(F, 16, vec).astype(f32)
    bias_output, gain_one, shift_one, bias_out, gain_two, shift_two = (
        smalls[:, i].reshape(width) for i in range(2, 8)
    )
    bias_in = smalls[:, 8 : 8 + fan].reshape(-1)
    tokens_single = tokens.astype(f32)
    attn_out = jnp.dot(mixed, wo, preferred_element_type=f32) + bias_output
    normed, pull_first = jax.vjp(layer_norm, tokens_single + attn_out, gain_one, shift_one)
    normed_low = normed.astype(bf16)
    hidden_pre = jnp.dot(normed_low, w1, preferred_element_type=f32) + bias_in
    hidden_single, pull_gelu = jax.vjp(gelu_exact, hidden_pre)
    hidden = hidden_single.astype(bf16)
    branch = jnp.dot(hidden, w2, preferred_element_type=f32) + bias_out
    layer_out, pull_second = jax.vjp(layer_norm, normed + branch, gain_two, shift_two)
    squares = jnp.stack(
        [jnp.sum(t * t) for t in (tokens_single, attn_out, normed, branch, layer_out)]
    )
    cotangent = out_cotangent.reshape(rows, width).astype(f32)
    grad_stream, grad_gain_two, grad_shift_two = pull_second(cotangent)
    grad_branch = grad_stream.astype(bf16)
    grad_bias_out = column_sums(grad_branch)
    grad_out = jnp.dot(hidden.T, grad_branch, preferred_element_type=f32)
    grad_hidden = jnp.dot(grad_branch, w2.T, preferred_element_type=f32)
    grad_pre = pull_gelu(grad_hidden)[0].astype(bf16)
    grad_bias_in = column_sums(grad_pre)
    grad_in = jnp.dot(normed_low.T, grad_pre, preferred_element_type=f32)
    grad_normed = grad_stream + jnp.dot(grad_pre, w1.T, preferred_element_type=f32)
    grad_h, grad_gain_one, grad_shift_one = pull_first(grad_normed)
    grad_attn = grad_h.astype(bf16)
    grad_bias_output = column_sums(grad_attn)
    grad_output = jnp.dot(mixed.T, grad_attn, preferred_element_type=f32)
    grad_mixed = jnp.dot(grad_attn, wo.T, preferred_element_type=f32).astype(bf16)
    grad_mixed = lax.all_to_all(grad_mixed, "seq", split_axis=1, concat_axis=0, tiled=True)
    length, wide = q.shape
    heads = wide // HD
    blocks = length // min(512, length)
    split = lambda t: t.reshape(length, heads, HD)
    keys, values = split(k), split(v)
    lse = lse[:heads].reshape(heads, blocks, length // blocks).swapaxes(0, 1)

    def backward_block(carry, parts):
        grad_keys, grad_values = carry
        query_block, total, grad_block = parts
        scores = jnp.einsum("qhd,khd->hqk", query_block, keys, preferred_element_type=f32)
        probs = jnp.exp(scores - total[..., None])
        grad_probs = jnp.einsum("qhd,khd->hqk", grad_block, values, preferred_element_type=f32)
        delta = jnp.sum(probs * grad_probs, axis=-1, keepdims=True)
        grad_scores = (probs * (grad_probs - delta)).astype(bf16)
        grad_query = jnp.einsum("hqk,khd->qhd", grad_scores, keys, preferred_element_type=f32) * 0.125
        grad_keys += jnp.einsum("hqk,qhd->khd", grad_scores, query_block, preferred_element_type=f32)
        grad_values += jnp.einsum("hqk,qhd->khd", probs.astype(bf16), grad_block, preferred_element_type=f32)
        return ((grad_keys, grad_values), grad_query.astype(bf16))

    in_blocks = lambda t: t.reshape(blocks, length // blocks, heads, HD)
    zero = jnp.zeros((length, heads, HD), f32)
    (grad_keys, grad_values), grad_queries = lax.scan(
        backward_block, (zero, zero), (in_blocks(q), lse, in_blocks(grad_mixed))
    )
    grad_q = grad_queries.reshape(length, wide)
    grad_k = grad_keys.reshape(length, wide).astype(bf16)
    grad_v = grad_values.reshape(length, wide).astype(bf16)
    grads = jnp.concatenate([grad_q, grad_k, grad_v], axis=1)
    input_part = jnp.dot(grads, wqkv.T, preferred_element_type=f32)
    input_grad = grad_h + lax.psum_scatter(input_part, "seq", scatter_dimension=0, tiled=True)
    grad_qkv = jnp.dot(xfull.T, grads, preferred_element_type=f32)

    def over_fsdp(t):
        return lax.psum_scatter(t, "fsdp", scatter_dimension=0, tiled=True)

    wide_sums = over_fsdp(grad_qkv.astype(bf16))
    wide_sums = lax.all_gather(wide_sums, "seq", axis=0, tiled=False).astype(f32)
    grad_query, grad_key, grad_value = (
        wide_sums[:, :, i * wide : (i + 1) * wide].swapaxes(0, 1).reshape(-1, width) for i in range(3)
    )
    weights = [
        lax.psum(over_fsdp(t.astype(bf16)), "seq").astype(f32) for t in (grad_output, grad_in, grad_out)
    ]
    bias_q = lax.all_gather(column_sums(grad_q), "seq", axis=0, tiled=True)
    bias_v = lax.all_gather(column_sums(grad_v), "seq", axis=0, tiled=True)
    sums = jnp.stack(
        [
            bias_q / S,
            bias_v / S,
            grad_bias_output,
            grad_gain_one,
            grad_shift_one,
            grad_bias_out,
            grad_gain_two,
            grad_shift_two,
        ]
    )
    f = lax.axis_index("fsdp")
    extra = jnp.zeros((1, width), f32).at[0, :5].set(squares)
    table = jnp.concatenate([sums, grad_bias_in.reshape(fan, width), extra])
    table = lax.psum(table, ("seq", "fsdp"))
    small_grads = lax.dynamic_slice_in_dim(table[:8], f * vec, vec, 1)
    grad_bias_in = lax.dynamic_slice_in_dim(table[8 : 8 + fan].reshape(-1), f * vec * fan, vec * fan, 0)
    rms = jnp.sqrt(table[8 + fan, :5] / f32(rows * width * S * F))
    return (
        layer_out.astype(bf16).reshape(layer_input.shape),
        input_grad.reshape(layer_input.shape),
        grad_query,
        grad_key,
        grad_value,
        weights[0],
        small_grads[0],
        small_grads[1],
        small_grads[2],
        small_grads[3],
        small_grads[4],
        weights[1],
        grad_bias_in,
        weights[2],
        small_grads[5],
        small_grads[6],
        small_grads[7],
        rms,
    )


def solution(mesh):
    placed = (
        P("fsdp", "seq", None),
        P("fsdp", None),
        P("fsdp", None),
        P("fsdp", None),
        P("fsdp", None),
        P("fsdp"),
        P("fsdp"),
        P("fsdp"),
        P("fsdp"),
        P("fsdp"),
        P("fsdp", None),
        P("fsdp"),
        P("fsdp", None),
        P("fsdp"),
        P("fsdp"),
        P("fsdp"),
        P("fsdp", "seq", None),
    )
    return jax.shard_map(
        local,
        mesh=mesh,
        in_specs=placed,
        out_specs=(
            P("fsdp", "seq", None),
            P("fsdp", "seq", None),
            P("fsdp", None),
            P("fsdp", None),
            P("fsdp", None),
            P("fsdp", None),
            P("fsdp"),
            P("fsdp"),
            P("fsdp"),
            P("fsdp"),
            P("fsdp"),
            P("fsdp", None),
            P("fsdp"),
            P("fsdp", None),
            P("fsdp"),
            P("fsdp"),
            P("fsdp"),
            P(),
        ),
        check_vma=False,
    )
```

time: 1660 us -> 779 us (0.47)
  waiting for transfers between devices: 1060 us -> 344 us
  blocking collectives: 253 us -> 61.1 us
  Pallas kernels: 0 us -> 128 us
  matrix products: 203 us -> 148 us
  local copies, waits for them, and re-layouts: 70.4 us -> 38 us
    reduce_scatter x6 -> x5, waiting for transfers between devices: 802 us -> 283 us  [the longest x4 234 us: over_fsdp(): return lax.psum_scatter(t, 'fsdp', scatter_dimension=0, tiled=True)]
    all_gather x6 -> x0, waiting for transfers between devices: 190 us -> none  [the longest x1 74.8 us: local(): lax.all_gather(out_weight, 'fsdp', axis=0, tiled=True)]
    pallas_call x0 -> x1, Pallas kernels: none -> 128 us  [forward(): pl.pallas_call(functools.partial(forward_kernel, plan), out_shape=(sds((l...]
    all_gather x9 -> x3, blocking collectives: 131 us -> 21.1 us  [the longest x1 10.4 us: local(): lax.all_gather(wide_sums, 'seq', axis=0, tiled=False).astype(f32)]
    dot_general x36 -> x23, matrix products: 186 us -> 131 us  [the longest x1 20.9 us: local(): hidden_pre = jnp.dot(normed_low, w1, preferred_element_type=f32) + bias_in]
    all_to_all x1 -> x0, blocking collectives: 39.7 us -> none  [local(): lax.all_to_all(grad_heads, 'seq', split_axis=1, concat_axis=2, tiled=True)]
    all_to_all x3 -> x1, waiting for transfers between devices: 41.7 us -> 5.09 us  [local(): lax.all_to_all(grad_mixed, 'seq', split_axis=1, concat_axis=0, tiled=True)]
    psum x1, waiting for transfers between devices: 26.7 us -> 55.6 us  [local(): lax.psum(over_fsdp(t.astype(bf16)), 'seq').astype(f32)]
  transfers between devices with their start and end apart: 16 -> 7, of which waited for: 12 -> 6; matrix products, arithmetic and copies ran while one was open for 15% -> 18% of each run, Pallas kernels for 0% -> 0%
where the time goes in v1:
time: 779 us; the launch traced here: 769 us
  waiting for transfers between devices  344 us (44%)
  matrix products  148 us (19%)
  Pallas kernels  128 us (16%)
  blocking collectives  61.1 us (8%)
  local copies, waits for them, and re-layouts  38 us (5%)
  other arithmetic  29.4 us (4%)
  between operations  15.1 us (2%)
    reduce_scatter x4, waiting for transfers between devices, over_fsdp(): return lax.psum_scatter(t, 'fsdp', scatter_dimension=0, tiled=True)  234 us
    pallas_call x1, Pallas kernels, forward(): pl.pallas_call(functools.partial(forward_kernel, plan), out_shape=(sds((l...  128 us
    psum x1, waiting for transfers between devices, local(): lax.psum(over_fsdp(t.astype(bf16)), 'seq').astype(f32)  55.6 us
    reduce_scatter x1, waiting for transfers between devices, local(): lax.psum_scatter(input_part, 'seq', scatter_dimension=0, tiled=True)  48.8 us
    psum x1, blocking collectives, local(): table = lax.psum(table, ('seq', 'fsdp'))  40 us
    dot_general x1, matrix products, local(): hidden_pre = jnp.dot(normed_low, w1, preferred_element_type=f32) + bias_in  20.9 us
    dot_general x3, matrix products, backward_block(): jnp.einsum('hqk,khd->qhd', grad_scores, keys, preferred_element_type=f32)  19 us
    dot_general x3, matrix products, backward_block(): jnp.einsum('hqk,qhd->khd', grad_scores, query_block, preferred_element_ty...  17 us
  transfers between devices with their start and end apart: 7, of which 6 were waited for; matrix products, arithmetic and copies ran while one was open for 18% of the time, Pallas kernels for 0%

profile of v1, /device:TPU:25, one launch (start us, length us, event | category | flops | bytes accessed | tf_op | source)
XLA Modules:
  0.0 769.3 jit_solution(2498052656960302895)
XLA Ops:
  12.6 128.4 %attention_forward_and_weight_gather.1 = (bf16[1536,1024]{1,0:T(8,128)(2,1)}, bf16[1024,768]{1,0:T(8,128)(2,1)}, bf16[128,128]{1,0:T(8,128)(2,1)S(1)}, bf16[1536...) custom-call(bf16[384,1024]{1,0:T(8,128)(2,1)} %bitcast.194, ...), custom_call_target="tpu_custom_call" | custom-call | tf_op jit(solution)/shard_map/attention_forward_and_weight_gather/pallas_call | solution.py:389
  141.0 3.8 fusion.57
  145.2 20.9 %multiply_convert_fusion.1 = (bf16[384,4096]{1,0:T(8,128)(2,1)S(1)}, f32[384,4096]{1,0:T(8,128)}, f32[384,4096]{1,0:T(8,128)}) fusion(f32[4096]{0:T(1024)S(1)} %bitcast.211, bf16[1024,4096]{1,0:T(8,128)(2,1)S(1)} %copy-done.28, f32[384,1024]{1,0:T(8,128)S(1)} %get-tuple-element.206, f32[1024]{0:T(1024)S(1)} %bitcast.219, f32[1024]{0:T(1024)S(1)} %bitcast.214, ...), kind=kOutput, calls=%fused_computation.35 | convolution fusion | flops 3327000576 | bytes 25717760 | tf_op jit(solution)/shard_map/dot_general | solution.py:487
  166.2 4.3 fusion.55
  174.5 13.5 %convert_reduce_fusion = (f32[4096]{0:T(1024)}, bf16[384,4096]{1,0:T(8,128)(2,1)S(1)}) fusion(f32[384,4096]{1,0:T(8,128)} %get-tuple-element.204, f32[384,4096]{1,0:T(8,128)} %get-tuple-element.230, bf16[384,1024]{1,0:T(8,128)(2,1)S(1)} %get-tuple-element.192, bf16[4096,1024]{1,0:T(8,128)(2,1)} %get-tuple-element.94), kind=kOutput, calls=%fused_computation.33 | convolution fusion | flops 3246387200 | bytes 24920064 | tf_op jit(solution)/shard_map/dot_general | solution.py:500
  188.0 4.5 multiply_reduce_fusion.5
  196.0 2.6 convolution_convert_fusion.2
  198.6 8.7 %convolution_convert_fusion = bf16[4096,1024]{1,0:T(8,128)(2,1)} fusion(bf16[384,4096]{1,0:T(8,128)(2,1)} %copy-done.32, bf16[384,1024]{1,0:T(8,128)(2,1)S(1)} %get-tuple-element.192), kind=kOutput, calls=%fused_computation.30 | convolution fusion | flops 3225419776 | bytes 12320768 | tf_op jit(solution)/shard_map/dot_general | solution.py:499
  207.6 10.4 %convolution_convert_fusion.1 = bf16[1024,4096]{1,0:T(8,128)(2,1)} fusion(bf16[384,4096]{1,0:T(8,128)(2,1)} %copy-done.31, f32[384,1024]{1,0:T(8,128)} %copy-done.14, f32[1024]{0:T(1024)S(1)} %bitcast.222, f32[1024]{0:T(1024)S(1)} %bitcast.218, f32[384]{0:T(512)S(1)} %fusion.45, f32[384]{0:T(512)S(1)} %broadcast_multiply_fusion.3), kind=kOutput, calls=%fused_computation.31 | convolution fusion | flops 3227385856 | bytes 13118464 | tf_op jit(solution)/shard_map/dot_general | solution.py:503
  218.0 2.9 convolution_convert_fusion.4
  222.1 4.3 all-to-all-start
  228.2 3.4 copy.57
  232.2 5.1 all-to-all-done
  237.3 2.7 copy.55
  239.9 2.6 reshape.295
  243.6 85.8 %while.16 = (s32[]{:T(128)}, f32[1536,4,64]{0,2,1:T(8,128)}, f32[1536,4,64]{0,2,1:T(8,128)}, bf16[3,512,4,64]{1,3,2,0:T(8,128)(2,1)}, bf16[3,512,4,64]{1,3,2,0:T...) while((s32[]{:T(128)}, f32[1536,4,64]{0,2,1:T(8,128)}, ...), condition=%wide.region_10.0_spmd.clone, body=%wide.region_8.10_spmd.clone.sunk | while | flops 2043410432 | bytes 217639696 | solution.py:533
  243.6 2.8 fusion.104
  246.4 4.0 multiply_reduce_fusion.10
  250.9 4.4 multiply_convert_fusion.3
  255.3 5.4 fusion.105
  260.7 6.3 fusion.107
  267.1 3.4 fusion.106
  271.6 2.8 fusion.104
  274.4 4.0 multiply_reduce_fusion.10
  279.5 4.4 multiply_convert_fusion.3
  283.9 5.8 fusion.105
  289.7 6.3 fusion.107
  296.0 3.4 fusion.106
  300.6 2.8 fusion.104
  303.4 4.0 multiply_reduce_fusion.10
  308.0 4.4 multiply_convert_fusion.3
  312.4 5.8 fusion.105
  318.2 6.3 fusion.107
  324.5 3.4 fusion.106
  333.4 3.8 convolution_convert_fusion.3
  337.2 6.1 fusion.42
  344.1 3.3 stack.43
  349.2 5.6 all-gather.2
  354.8 5.1 all-gather.1
  360.0 40.0 %psum.29 = f32[13,1024]{1,0:T(8,128)S(1)} all-reduce(f32[13,1024]{1,0:T(8,128)S(1)} %concatenate.18), channel_id=1, replica_groups=mesh['seq'=4,'fsdp'=8] {'seq','fsdp'}, use_global_device_ids=true, to_apply=%region_30.31 | all-reduce | flops 13312 | bytes 106496 | tf_op jit(solution)/shard_map/psum | solution.py:572
  400.6 16.6 %reduce-scatter.14.cloned.1.call-done = bf16[512,1024]{1,0:T(8,128)(2,1)} async-done(((bf16[4096,1024]{1,0:T(8,128)(2,1)}), bf16[512,1024]{1,0:T(8,128)(2,1)}) %reduce-scatter.14.cloned.1.call-update) | async-done | bytes 1048592 | tf_op jit(solution)/shard_map/reduce_scatter | solution.py:545
  417.2 151.9 %reduce-scatter.12.cloned.1.call-done = bf16[128,4096]{1,0:T(8,128)(2,1)} async-done(((bf16[1024,4096]{1,0:T(8,128)(2,1)}), bf16[128,4096]{1,0:T(8,128)(2,1)}) %reduce-scatter.12.cloned.1.call-update) | async-done | bytes 1048592 | tf_op jit(solution)/shard_map/reduce_scatter | solution.py:545
  570.3 65.9 %reduce-scatter.8.cloned.1.call-done = bf16[128,768]{1,0:T(8,128)(2,1)} async-done(((bf16[1024,768]{1,0:T(8,128)(2,1)}), bf16[128,768]{1,0:T(8,128)(2,1)}) %reduce-scatter.8.cloned.1.call-update) | async-done | bytes 196624 | tf_op jit(solution)/shard_map/reduce_scatter | solution.py:545
  636.2 10.4 %all-gather = bf16[512,768]{1,0:T(8,128)(2,1)S(1)} all-gather(bf16[128,768]{1,0:T(8,128)(2,1)} %reduce-scatter.8.cloned.1.call-done), channel_id=2, replica_groups=mesh['seq'=4,'fsdp'=8] {'seq'}, dimensions={0}, use_global_device_ids=true | all-gather | bytes 983040 | tf_op jit(solution)/shard_map/all_gather | solution.py:548
  649.5 48.8 %reduce-scatter.6.cloned.1.call-done = f32[384,1024]{1,0:T(8,128)} async-done(((f32[1536,1024]{1,0:T(8,128)}), f32[384,1024]{1,0:T(8,128)}) %reduce-scatter.6.cloned.1.call-update) | async-done | bytes 1572880 | tf_op jit(solution)/shard_map/reduce_scatter | solution.py:541
  698.3 2.8 add_bitcast_fusion
  701.1 55.6 %all-reduce.4.cloned.1.call-done = (bf16[128,1024]{1,0:T(8,128)(2,1)}, bf16[128,4096]{1,0:T(8,128)(2,1)}, bf16[512,1024]{1,0:T(8,128)(2,1)}) async-done(((bf16[128,1024]{1,0:T(8,128)(2,1)}, bf16[128,4096]{1,0:T(8,128)(2,1)}, bf16[512,1024]{1,0:T(8,128)(2,1)}), (bf16[128,1024]{1,0:T(8,128)(2,1)}, bf16[128,4096]{1,0:T(8,128)(2,1)}, bf16[512,1024]{1,0:T(8,128)(2,1)})) %all-reduce.4.cloned.1.call-update) | async-done | bytes 2359312 | tf_op jit(solution)/shard_map/psum | solution.py:553
  756.7 2.9 convert_element_type.128
  (160 shorter events, 37.4 us)
Async XLA Ops:
  7.2 393.4 %reduce-scatter.10.cloned.1.call-start = ((), (), s32[]{:S(2)}) async-start(), calls=%async_computation.8 | async-start | bytes 2359296 | tf_op jit(solution)/shard_map/reduce_scatter | solution.py:545
  8.7 0.9 copy-start
  9.7 0.9 copy-start.1
  10.7 0.9 copy-start.2
  11.6 0.9 copy-start.3
  12.6 128.4 %copy-start.17 = (bf16[1,384,1024]{2,1,0:T(8,128)(2,1)S(1)}, bf16[1,384,1024]{2,1,0:T(8,128)(2,1)}, u32[]{:S(2)}) copy-start(bf16[1,384,1024]{2,1,0:T(8,128)(2,1)} %param.21) | copy-start | bytes 2359300
  141.0 4.2 copy-start.28
  141.0 25.2 %slice-start = ((s8[8388608]{0:T(1024)(128)(4,1)}), s8[4194304]{0:T(1024)(128)(4,1)S(1)}, s32[]{:S(2)}) async-start(s8[8388608]{0:T(1024)(128)(4,1)} %bitcast.236), calls=%async_computation.12 | async-start | bytes 8388608
  144.8 47.8 %copy-start.14 = (f32[384,1024]{1,0:T(8,128)}, f32[384,1024]{1,0:T(8,128)S(1)}, u32[]{:S(2)}) copy-start(f32[384,1024]{1,0:T(8,128)S(1)} %get-tuple-element.206) | copy-start | bytes 4718596
  145.2 20.9 %slice-start.1 = ((s8[8388608]{0:T(1024)(128)(4,1)}), s8[4194304]{0:T(1024)(128)(4,1)S(1)}, s32[]{:S(2)}) async-start(s8[8388608]{0:T(1024)(128)(4,1)} %bitcast.236), calls=%async_computation.13 | async-start | bytes 8388608
  166.1 4.3 copy-start.32
  166.2 4.6 copy-start.12
  188.0 4.5 copy-start.31
  192.5 3.4 copy-start.30
  193.1 1.1 copy-start.10
  193.1 1.9 copy-start.20
  198.6 218.6 %reduce-scatter.14.cloned.1.call-start = ((), (), s32[]{:S(2)}) async-start(), calls=%async_computation.10 | async-start | bytes 9437184 | tf_op jit(solution)/shard_map/reduce_scatter | solution.py:545
  207.4 361.7 %reduce-scatter.12.cloned.1.call-start = ((), (), s32[]{:S(2)}) async-start(), calls=%async_computation.9 | async-start | bytes 9437184 | tf_op jit(solution)/shard_map/reduce_scatter | solution.py:545
  222.1 15.2 %all-to-all-start = ((bf16[384,4,256]{0,2,1:T(8,128)(2,1)}), bf16[384,4,256]{0,2,1:T(8,128)(2,1)}, u32[]{:S(2)}, u32[]{:S(2)}) async-start(bf16[384,4,256]{0,2,1:T(8,128)(2,1)} %bitcast.24), calls=%async_computation | async-start | bytes 1572864 | tf_op jit(solution)/shard_map/all_to_all | solution.py:510
  226.4 409.8 %reduce-scatter.8.cloned.1.call-start = ((), (), s32[]{:S(2)}) async-start(), calls=%async_computation.7 | async-start | bytes 1769472 | tf_op jit(solution)/shard_map/reduce_scatter | solution.py:545
  246.4 4.6 copy-start.4
  255.3 11.7 %copy-start.5 = (f32[4,512,1536]{2,1,0:T(8,128)S(1)}, f32[4,512,1536]{2,1,0:T(8,128)}, u32[]{:S(2)}) copy-start(f32[4,512,1536]{2,1,0:T(8,128)} %copy-done.4) | copy-start | bytes 37748740 | tf_op jit(solution)/shard_map/while
  260.7 6.3 copy-start.7
  270.5 1.1 copy-start.8
  274.4 5.1 copy-start.4
  283.9 12.2 %copy-start.5 = (f32[4,512,1536]{2,1,0:T(8,128)S(1)}, f32[4,512,1536]{2,1,0:T(8,128)}, u32[]{:S(2)}) copy-start(f32[4,512,1536]{2,1,0:T(8,128)} %copy-done.4) | copy-start | bytes 37748740 | tf_op jit(solution)/shard_map/while
  289.7 6.3 copy-start.7
  299.4 1.1 copy-start.8
  303.4 4.6 copy-start.4
  312.4 12.1 %copy-start.5 = (f32[4,512,1536]{2,1,0:T(8,128)S(1)}, f32[4,512,1536]{2,1,0:T(8,128)}, u32[]{:S(2)}) copy-start(f32[4,512,1536]{2,1,0:T(8,128)} %copy-done.4) | copy-start | bytes 37748740 | tf_op jit(solution)/shard_map/while
  318.2 6.3 copy-start.7
  328.0 1.1 copy-start.8
  329.4 2.2 copy-start.6
  329.4 2.3 copy-start.9
  331.4 2.0 copy-start.29
  337.2 361.1 %reduce-scatter.6.cloned.1.call-start = ((), (), s32[]{:S(2)}) async-start(), calls=%async_computation.6 | async-start | bytes 7864320 | tf_op jit(solution)/shard_map/reduce_scatter | solution.py:541
  343.3 5.4 copy-start.13
  343.3 5.6 copy-start.15
  343.3 16.5 %copy-start.22 = (f32[1024]{0:T(1024)S(1)}, f32[1024]{0:T(1024)}, u32[]{:S(2)}) copy-start(f32[1024]{0:T(1024)} %get-tuple-element.163) | copy-start | bytes 12292
  343.3 16.5 %copy-start.23 = (f32[1024]{0:T(1024)S(1)}, f32[1024]{0:T(1024)}, u32[]{:S(2)}) copy-start(f32[1024]{0:T(1024)} %get-tuple-element.191) | copy-start | bytes 12292
  343.4 16.5 %copy-start.24 = (f32[1024]{0:T(1024)S(1)}, f32[1024]{0:T(1024)}, u32[]{:S(2)}) copy-start(f32[1024]{0:T(1024)} %get-tuple-element.193) | copy-start | bytes 12292
  343.4 16.5 %copy-start.26 = (f32[1024]{0:T(1024)S(1)}, f32[1024]{0:T(1024)}, u32[]{:S(2)}) copy-start(f32[1024]{0:T(1024)} %get-tuple-element.161) | copy-start | bytes 12292
  343.4 16.5 %copy-start.27 = (f32[1024]{0:T(1024)S(1)}, f32[1024]{0:T(1024)}, u32[]{:S(2)}) copy-start(f32[1024]{0:T(1024)} %get-tuple-element.167) | copy-start | bytes 12292
  343.4 413.3 %all-reduce.4.cloned.1.call-start = ((), (), s32[]{:S(2)}) async-start(), calls=%async_computation.11 | async-start | bytes 4718592 | tf_op jit(solution)/shard_map/psum | solution.py:553
  646.8 51.5 %copy-start.11 = (f32[384,1024]{1,0:T(8,128)S(1)}, f32[384,1024]{1,0:T(8,128)}, u32[]{:S(2)}) copy-start(f32[384,1024]{1,0:T(8,128)} %copy-done.10) | copy-start | bytes 4718596
  646.8 51.5 %copy-start.21 = (f32[384]{0:T(512)S(1)}, f32[384]{0:T(512)}, u32[]{:S(2)}) copy-start(f32[384]{0:T(512)} %copy-done.20) | copy-start | bytes 4612
  756.7 2.9 copy-start.16
  756.7 4.4 copy-start.19
  (2 other events, 1.6 us)
Sparse Core Ops, SparseCore 0:
  198.7 64.3 reduce-scatter.9
  266.8 150.3 reduce-scatter.13
  421.2 147.7 reduce-scatter.11
  572.9 63.2 reduce-scatter.7
  638.8 59.4 reduce-scatter.5
  700.7 55.9 all-reduce.3

commit v2 on v1

--- a/solution.py
+++ b/solution.py
@@ -425,6 +425,478 @@
         compiler_params=pltpu.CompilerParams(collective_id=0, has_side_effects=True, vmem_limit_bytes=48 << 20),
         name="attention_forward_and_weight_gather",
     )(x, wq, wk, wv, small, wo, w1, w2)
+
+
+class Reduce:
+    def __init__(self, alloc, S, F, Y, R, C, kind):
+        self.kind, self.R, self.C = kind, R, C
+        self.S, self.F, self.Y, self.Z, self.H = S, F, Y, F // Y, S // 2
+        Z, H = self.Z, self.H
+        self.w = {"half": C // 2, "quarter": C // S, "own": C}[kind]
+        w = self.w
+        self.n = H if kind == "quarter" else 1
+        self.shapes = [(self.n, Z, Y, R, w), (Y - 1, Z, R, w), (Z, R, w)]
+        if kind == "own":
+            self.shapes += [(S, R, w)]
+        else:
+            self.shapes += [(self.n, Z, Y, R, w), (R, C)]
+            self.shapes += [(H - 1, Z, Y, R, w) if kind == "quarter" else (H - 1, R, w)]
+        self.shapes = [pltpu.VMEM(s, bf16) for s in self.shapes]
+        self.load = alloc.take(H)
+        self.ds, self.dr = alloc.take(H), alloc.take(H)
+        self.xs, self.xr = alloc.take(H), alloc.take(H)
+        self.ys, self.yr = alloc.take(Y), alloc.take(Y)
+        self.zs, self.zr = alloc.take(Z), alloc.take(Z)
+        self.fs, self.fr = alloc.take(2 * H), alloc.take(2 * H)
+        self.out = alloc.take(1)
+
+    def bind(self, g, sems, refs, source, dest):
+        self.g, self.sems, self.source, self.dest = g, sems, source, dest
+        if self.kind == "own":
+            self.own, self.ry, self.rz, self.fin = refs
+        else:
+            self.own, self.ry, self.rz, self.rd, self.fin, self.rx = refs
+        self.sends = []
+
+    def send(self, src, dst, s, r, to):
+        copy = rcopy(self.sems, src, dst, s, r, to)
+        copy.start()
+        self.sends.append(copy)
+
+    def recv(self, ref, r):
+        rcopy(self.sems, ref, ref, r, r, (self.g.sib(), self.g.f)).wait_recv()
+
+    def column(self, hi, c):
+        return (hi * 2 + c) * self.w if self.kind == "quarter" else c * self.w
+
+    def start(self):
+        g = self.g
+        self.loads = []
+        for m in range(self.n):
+            hi = (g.hi + m) % g.H
+            self.send(
+                self.source(self.column(hi, 1 - g.c), self.w),
+                self.rd.at[m],
+                self.ds + m,
+                self.dr + m,
+                (g.sib(), g.f),
+            )
+            copy = pltpu.make_async_copy(
+                self.source(self.column(hi, g.c), self.w), self.own.at[m], self.sems.at[self.load + m]
+            )
+            copy.start()
+            self.loads.append(copy)
+
+    def add_all(self, m, other):
+        @pl.loop(0, self.Z * self.Y)
+        def _(i):
+            a, b = i // self.Y, i % self.Y
+            self.own[m, a, b] = (self.own[m, a, b].astype(f32) + other(a, b).astype(f32)).astype(bf16)
+
+    def over_cores(self):
+        for m in list(range(1, self.n)) + [0]:
+            self.loads[m].wait()
+            self.recv(self.rd.at[m], self.dr + m)
+            self.add_all(m, lambda a, b: self.rd[m, a, b])
+            if m:
+                self.send(self.own.at[m], self.rx.at[m - 1], self.xs + m, self.xr + m, (self.g.xp(m), self.g.f))
+        if self.kind == "half":
+            self.send_y()
+
+    def over_x_first(self):
+        for m in range(1, self.H):
+            self.recv(self.rx.at[m - 1], self.xr + m)
+            self.add_all(0, lambda a, b: self.rx[m - 1, a, b])
+        self.send_y()
+
+    def send_y(self):
+        g = self.g
+        for j in range(1, g.Y):
+            y = (g.y + j) % g.Y
+            self.send(self.own.at[0, :, y], self.ry.at[j - 1], self.ys + j, self.yr + j, (g.s, g.yp(j)))
+
+    def over_y(self):
+        g = self.g
+        for j in range(1, g.Y):
+            self.recv(self.ry.at[j - 1], self.yr + j)
+
+        @pl.loop(0, self.Z)
+        def _(a):
+            total = self.own[0, a, g.y].astype(f32)
+            for j in range(1, g.Y):
+                total += self.ry[j - 1, a].astype(f32)
+            self.own[0, a, g.y] = total.astype(bf16)
+
+        for k in range(1, g.Z):
+            z = (g.z + k) % g.Z
+            self.send(self.own.at[0, z, g.y], self.rz.at[k], self.zs + k, self.zr + k, (g.s, g.zp(k)))
+
+    def over_z(self):
+        g = self.g
+        total = self.own[0, g.z, g.y].astype(f32)
+        for k in range(1, g.Z):
+            self.recv(self.rz.at[k], self.zr + k)
+            total += self.rz[k].astype(f32)
+        total = total.astype(bf16)
+        if self.kind == "half":
+            self.rz[0] = total
+            for m in range(1, g.H):
+                self.send(self.rz.at[0], self.rx.at[m - 1], self.xs + m, self.xr + m, (g.xp(m), g.f))
+            return
+        if self.kind == "own":
+            self.fin[g.s] = total
+            ref = self.fin.at[g.s]
+        else:
+            at = pl.multiple_of(self.column(g.hi, g.c), self.w)
+            self.fin[:, pl.ds(at, self.w)] = total
+            ref = self.fin.at[:, pl.ds(at, self.w)]
+        for m in range(1, g.H):
+            self.send(ref, ref, self.fs + m, self.fr + m, (g.xp(m), g.f))
+        self.send(ref, ref, self.fs, self.fr, (g.sib(), g.f))
+
+    def over_x_last(self):
+        g = self.g
+        if self.kind == "half":
+            total = self.rz[0].astype(f32)
+            for m in range(1, g.H):
+                self.recv(self.rx.at[m - 1], self.xr + m)
+                total += self.rx[m - 1].astype(f32)
+            at = pl.multiple_of(g.c * self.w, self.w)
+            self.fin[:, pl.ds(at, self.w)] = total.astype(bf16)
+            ref = self.fin.at[:, pl.ds(at, self.w)]
+            self.send(ref, ref, self.fs, self.fr, (g.sib(), g.f))
+            return
+        for m in range(1, g.H):
+            hi = (g.hi + g.H - m) % g.H
+            if self.kind == "own":
+                ref = self.fin.at[hi * 2 + g.c]
+            else:
+                ref = self.fin.at[:, pl.ds(self.column(hi, g.c), self.w)]
+            self.recv(ref, self.fr + m)
+            self.send(ref, ref, self.fs + g.H + m, self.fr + g.H + m, (g.sib(), g.f))
+
+    def finish(self):
+        g = self.g
+        for m in range(g.H if self.kind != "half" else 1):
+            hi = (g.hi + g.H - m) % g.H
+            if self.kind == "own":
+                ref = self.fin.at[hi * 2 + 1 - g.c]
+            else:
+                ref = self.fin.at[:, pl.ds(self.column(hi, 1 - g.c), self.w)]
+            self.recv(ref, self.fr + (g.H + m if m else 0))
+        self.copy_out = pltpu.make_async_copy(self.fin, self.dest, self.sems.at[self.out])
+        self.copy_out.start()
+
+    def done(self):
+        for copy in self.sends:
+            copy.wait_send()
+        self.copy_out.wait()
+
+    def steps(self):
+        if self.kind == "half":
+            return [self.over_y, self.over_z, self.over_x_last, self.finish]
+        if self.kind == "quarter":
+            return [self.over_x_first, self.over_y, self.over_z, self.over_x_last, self.finish]
+        return [self.over_y, self.over_z, self.over_x_last, self.finish]
+
+
+def backward_kernel(plan, g_o, q_i, k_i, v_i, qt_i, kt_i, ot_i, lse_i, x_i, w_i, gh, table_i, dwo, dw1, dw2, *rest):
+    dx_o, dqkv_o, dwo_o, dw1_o, dw2_o, table_o = rest[:6]
+    (go, qn, kn, vn, qt, kt, ot, lse, xs, ws, dk, dv, dqt, dt, delta, grads) = rest[6:22]
+    (dx, dx_send, dx_core, dx_out, dx_x, tab, tab_core, tab_x, tab_y, tab_s, tab_z, sems) = rest[22:34]
+    pools = rest[34:]
+    S, F, rows, heads, wide, vec = plan.S, plan.F, plan.rows, plan.heads, plan.wide, plan.vec
+    g = Grid(S, F)
+    g.greet(pltpu.get_barrier_semaphore())
+
+    def keep(src, dst, at):
+        copy = pltpu.make_async_copy(src, dst, sems.at[at])
+        copy.start()
+        return copy
+
+    sent = []
+
+    def send(src, dst, s, r, to):
+        copy = rcopy(sems, src, dst, s, r, to)
+        copy.start()
+        sent.append(copy)
+
+    def recv(ref, r):
+        rcopy(sems, ref, ref, r, r, (g.sib(), g.f)).wait_recv()
+
+    for m in [*range(1, g.H), 0]:
+        for flip in range(2):
+            if m or flip:
+                to = ((g.hi + m) % g.H) * 2 + (g.c + flip) % 2
+                send(
+                    g_o.at[:, pl.ds(to * wide, wide)],
+                    go.at[g.s],
+                    plan.o_s + m * 2 + flip,
+                    plan.o_r + g.s,
+                    (to, g.f),
+                )
+    used = 0
+    for item, which, col, row in plan.items:
+        n = len(item.shapes)
+        src, dst = {"o": (dwo, dwo_o), "1": (dw1, dw1_o), "2": (dw2, dw2_o)}[which]
+        item.bind(
+            g,
+            sems,
+            pools[used : used + n],
+            lambda lo, width, src=src, item=item, col=col, row=row: src.at[
+                :, :, pl.ds(row, item.R), pl.ds(col + lo, width)
+            ],
+            dst.at[pl.ds(row, item.R), pl.ds(col, item.C)],
+        )
+        used += n
+        item.start()
+    plan.qkv.bind(g, sems, pools[used : used + 4], None, dqkv_o)
+    loads = [
+        keep(src, dst, plan.l + i)
+        for i, (src, dst) in enumerate(
+            (
+                (g_o.at[:, pl.ds(g.s * wide, wide)], go.at[g.s]),
+                (q_i, qn),
+                (k_i, kn),
+                (v_i, vn),
+                (qt_i, qt),
+                (kt_i, kt),
+                (ot_i, ot),
+                (lse_i, lse),
+                (x_i, xs),
+                (w_i, ws),
+                (gh, dx),
+                (table_i, tab),
+            )
+        )
+    ]
+    items = [entry[0] for entry in plan.items]
+    for item in items:
+        item.over_cores()
+    waves = []
+    for tick in range(len(items) + 5):
+        for i, item in enumerate(items):
+            steps = item.steps()
+            if 0 <= tick - i < len(steps):
+                waves.append((tick, steps[tick - i]))
+
+    def run(upto):
+        while waves and waves[0][0] <= upto:
+            waves.pop(0)[1]()
+
+    dk[...] = jnp.zeros_like(dk)
+    dv[...] = jnp.zeros_like(dv)
+    for copy in loads:
+        copy.wait()
+    for i in range(1, S):
+        peer = (g.s + i) % S
+        recv(go.at[peer], plan.o_r + peer)
+    head_of = lax.broadcasted_iota(jnp.int32, (wide, rows), 0) // HD
+    head_at = lax.broadcasted_iota(jnp.int32, (rows, wide), 1) // HD
+    none = jnp.zeros((), bf16)
+    for t in range(S):
+        span = pl.ds(t * rows, rows)
+        turned = go[t].astype(f32).T
+        dt[...] = turned.astype(bf16)
+        weighed = turned * ot[:, span].astype(f32)
+        for h in range(heads):
+            delta[pl.ds(h, 1), :] = jnp.sum(weighed[h * HD : (h + 1) * HD], axis=0, keepdims=True)
+
+        @pl.loop(0, heads)
+        def _(h):
+            band = pl.ds(pl.multiple_of(h * HD, HD), HD)
+            s = jnp.dot(kn[...], jnp.where(head_of == h, qt[:, span], none), preferred_element_type=f32)
+            p = jnp.exp(s - lse[pl.ds(h, 1), span])
+            dp = jnp.dot(vn[...], jnp.where(head_of == h, dt[...], none), preferred_element_type=f32)
+            ds = (p * (dp - delta[pl.ds(h, 1), :])).astype(bf16)
+            dv[...] += jnp.dot(p.astype(bf16), jnp.where(head_at == h, go[t], none), preferred_element_type=f32)
+            dk[...] += jnp.dot(ds, jnp.where(head_at == h, qn[span, :], none), preferred_element_type=f32)
+            dqt[band, span] = jnp.dot(kt[band, :], ds, preferred_element_type=f32) * 0.125
+
+        run(plan.ticks[t])
+
+    sum_q = jnp.zeros((1, wide), f32)
+    sum_v = jnp.zeros((1, wide), f32)
+    for t in range(S):
+        span = pl.ds(t * rows, rows)
+        q = dqt[:, span].T.astype(bf16)
+        v = dv[span, :].astype(bf16)
+        grads[span, pl.ds(0, wide)] = q
+        grads[span, pl.ds(wide, wide)] = dk[span, :].astype(bf16)
+        grads[span, pl.ds(2 * wide, wide)] = v
+        sum_q += jnp.sum(q.astype(f32), axis=0, keepdims=True)
+        sum_v += jnp.sum(v.astype(f32), axis=0, keepdims=True)
+    Y, part_rows, width = g.Y, plan.qkv.R, xs.shape[1]
+    step = max(part_rows, 256)
+    for lo in range(0, width, step):
+        prod = lax.dot_general(
+            xs[:, pl.ds(lo, step)], grads[...], (((0,), (0,)), ((), ())), preferred_element_type=f32
+        ).astype(bf16)
+        for i in range(step // part_rows):
+            to = lo // part_rows + i
+            plan.qkv.own[0, to // Y, to % Y] = prod[i * part_rows : (i + 1) * part_rows]
+    plan.qkv.send_y()
+    def part(to):
+        return lax.dot_general(
+            grads[pl.ds(pl.multiple_of(to * rows, rows), rows), :],
+            ws[...],
+            (((1,), (1,)), ((), ())),
+            preferred_element_type=f32,
+        )
+
+    for m in [*range(1, g.H), 0]:
+        hi = (g.hi + m) % g.H
+        dx_send[m] = part(hi * 2 + 1 - g.c).astype(bf16)
+        send(dx_send.at[m], dx_core.at[m], plan.dx + m, plan.dx + g.H + m, (g.sib(), g.f))
+    for m in [*range(1, g.H), 0]:
+        hi = (g.hi + m) % g.H
+        value = part(hi * 2 + g.c)
+        recv(dx_core.at[m], plan.dx + g.H + m)
+        value += dx_core[m].astype(f32)
+        if m:
+            dx_out[m - 1] = value.astype(bf16)
+            send(dx_out.at[m - 1], dx_x.at[m - 1], plan.dx + 2 * g.H + m, plan.dx + 3 * g.H + m, (g.xp(m), g.f))
+        else:
+            dx[...] += value
+    base = g.s * (wide // vec)
+    for i in range(wide // vec):
+        to = base + i
+        for row, value in ((0, sum_q), (1, sum_v)):
+            tab[to // Y, to % Y, pl.ds(row, 1), :] = value[:, i * vec : (i + 1) * vec]
+    send(tab, tab_core, plan.t, plan.t + 1, (g.sib(), g.f))
+    recv(tab_core, plan.t + 1)
+    tab_x[g.hi] = tab[...] + tab_core[...]
+    for m in range(1, g.H):
+        send(tab_x.at[g.hi], tab_x.at[g.hi], plan.tx + m, plan.tx + g.H + g.hi, (g.xp(m), g.f))
+    for m in range(1, g.H):
+        hi = (g.hi + m) % g.H
+        recv(tab_x.at[hi], plan.tx + g.H + hi)
+    total = tab_x[0]
+    for m in range(1, g.H):
+        total += tab_x[m]
+    tab_core[...] = total
+    tab_y[g.y] = tab_core[:, g.y]
+    for j in range(1, Y):
+        y = (g.y + j) % Y
+        send(tab_core.at[:, y], tab_y.at[g.y], plan.ty + j, plan.ty + Y + g.y, (g.s, g.yp(j)))
+    for j in range(1, Y):
+        y = (g.y + j) % Y
+        recv(tab_y.at[y], plan.ty + Y + y)
+    total = tab_y[0]
+    for j in range(1, Y):
+        total += tab_y[j]
+    tab_s[...] = total
+    tab_z[g.z] = tab_s[g.z]
+    for k in range(1, g.Z):
+        z = (g.z + k) % g.Z
+        send(tab_s.at[z], tab_z.at[g.z], plan.tz + k, plan.tz + g.Z + g.z, (g.s, g.zp(k)))
+    run(plan.ticks[S])
+    for k in range(1, g.Z):
+        z = (g.z + k) % g.Z
+        recv(tab_z.at[z], plan.tz + g.Z + z)
+    total = tab_z[0]
+    for k in range(1, g.Z):
+        total += tab_z[k]
+    tab_y[0, 0] = total
+    out = [keep(tab_y.at[0, 0], table_o, plan.l + 12)]
+    ending = plan.qkv.steps()
+    for i, step_of in enumerate(ending):
+        run(plan.ticks[S] + 1 + i)
+        step_of()
+    run(1000)
+    for m in range(1, g.H):
+        recv(dx_x.at[m - 1], plan.dx + 3 * g.H + m)
+        dx[...] += dx_x[m - 1].astype(f32)
+    out.append(keep(dx, dx_o, plan.l + 13))
+    for item in (*items, plan.qkv):
+        item.done()
+    for copy in sent:
+        copy.wait_send()
+    for copy in out:
+        copy.wait()
+
+
+def backward_plan(S, F, rows, width, ff):
+    plan = Plan()
+    alloc = Sems()
+    plan.S, plan.F, plan.rows = S, F, rows
+    plan.wide = width // S
+    plan.heads = plan.wide // HD
+    plan.vec = width // F
+    Y = 2 if F % 2 == 0 and F <= 8 else 4
+    R, R2 = width // F, ff // F
+    ones = [(Reduce(alloc, S, F, Y, R, width, "quarter"), "1", i * width, 0) for i in range(ff // width)]
+    twos = [(Reduce(alloc, S, F, Y, R2 // 4, width, "half"), "2", 0, i * (R2 // 4)) for i in range(4)]
+    plan.items = [e for pair in zip(twos, ones) for e in pair]
+    plan.items.append((Reduce(alloc, S, F, Y, R, width, "half"), "o", 0, 0))
+    plan.qkv = Reduce(alloc, S, F, Y, R, 3 * plan.wide, "own")
+    plan.o_s, plan.o_r = alloc.take(S), alloc.take(S)
+    plan.dx = alloc.take(4 * S)
+    plan.t, plan.tx, plan.ty, plan.tz = alloc.take(2), alloc.take(S), alloc.take(2 * Y), alloc.take(2 * F // Y)
+    plan.l = alloc.take(14)
+    plan.ticks = [1, 3, 5, 7, 9]
+    plan.sems = alloc.n
+    return plan
+
+
+def backward(S, F, g_o, q, k, v, qt, kt, ot, lse, x, w, gh, table, dwo, dw1, dw2):
+    rows, width = g_o.shape
+    ff = dw1.shape[-1]
+    plan = backward_plan(S, F, rows, width, ff)
+    wide, vec = plan.wide, plan.vec
+    length = rows * S
+    Z, Y = table.shape[:2]
+    H = S // 2
+    R, R2 = width // F, ff // F
+    sds = jax.ShapeDtypeStruct
+    any_ = pl.BlockSpec(memory_space=pl.ANY)
+    pools = [s for e in plan.items for s in e[0].shapes] + plan.qkv.shapes
+    return pl.pallas_call(
+        functools.partial(backward_kernel, plan),
+        out_shape=(
+            sds((rows, width), f32),
+            sds((S, R, 3 * wide), bf16),
+            sds((R, width), bf16),
+            sds((R, ff), bf16),
+            sds((R2, width), bf16),
+            sds((16, vec), f32),
+        ),
+        in_specs=[any_] * 15,
+        out_specs=(any_,) * 6,
+        scratch_shapes=[
+            pltpu.VMEM((S, rows, wide), bf16),
+            pltpu.VMEM((length, wide), bf16),
+            pltpu.VMEM((length, wide), bf16),
+            pltpu.VMEM((length, wide), bf16),
+            pltpu.VMEM((wide, length), bf16),
+            pltpu.VMEM((wide, length), bf16),
+            pltpu.VMEM((wide, length), bf16),
+            pltpu.VMEM((8, length), f32),
+            pltpu.VMEM((length, width), bf16),
+            pltpu.VMEM((width, 3 * wide), bf16),
+            pltpu.VMEM((length, wide), f32),
+            pltpu.VMEM((length, wide), f32),
+            pltpu.VMEM((wide, length), f32),
+            pltpu.VMEM((wide, rows), bf16),
+            pltpu.VMEM((8, rows), f32),
+            pltpu.VMEM((length, 3 * wide), bf16),
+            pltpu.VMEM((rows, width), f32),
+            pltpu.VMEM((H, rows, width), bf16),
+            pltpu.VMEM((H, rows, width), bf16),
+            pltpu.VMEM((H - 1, rows, width), bf16),
+            pltpu.VMEM((H - 1, rows, width), bf16),
+            pltpu.VMEM((Z, Y, 16, vec), f32),
+            pltpu.VMEM((Z, Y, 16, vec), f32),
+            pltpu.VMEM((H, Z, Y, 16, vec), f32),
+            pltpu.VMEM((Y, Z, 16, vec), f32),
+            pltpu.VMEM((Z, 16, vec), f32),
+            pltpu.VMEM((Z, 16, vec), f32),
+            pltpu.SemaphoreType.DMA((plan.sems,)),
+            *pools,
+        ],
+        compiler_params=pltpu.CompilerParams(collective_id=1, has_side_effects=True, vmem_limit_bytes=63 << 20),
+        name="attention_backward_and_gradient_sums",
+    )(g_o, q, k, v, qt, kt, ot, lse, x, w, gh, table, dwo, dw1, dw2)
 
 
 def layer_norm(stream, gain, shift):
@@ -507,72 +979,46 @@
     grad_bias_output = column_sums(grad_attn)
     grad_output = jnp.dot(mixed.T, grad_attn, preferred_element_type=f32)
     grad_mixed = jnp.dot(grad_attn, wo.T, preferred_element_type=f32).astype(bf16)
-    grad_mixed = lax.all_to_all(grad_mixed, "seq", split_axis=1, concat_axis=0, tiled=True)
-    length, wide = q.shape
-    heads = wide // HD
-    blocks = length // min(512, length)
-    split = lambda t: t.reshape(length, heads, HD)
-    keys, values = split(k), split(v)
-    lse = lse[:heads].reshape(heads, blocks, length // blocks).swapaxes(0, 1)
-
-    def backward_block(carry, parts):
-        grad_keys, grad_values = carry
-        query_block, total, grad_block = parts
-        scores = jnp.einsum("qhd,khd->hqk", query_block, keys, preferred_element_type=f32)
-        probs = jnp.exp(scores - total[..., None])
-        grad_probs = jnp.einsum("qhd,khd->hqk", grad_block, values, preferred_element_type=f32)
-        delta = jnp.sum(probs * grad_probs, axis=-1, keepdims=True)
-        grad_scores = (probs * (grad_probs - delta)).astype(bf16)
-        grad_query = jnp.einsum("hqk,khd->qhd", grad_scores, keys, preferred_element_type=f32) * 0.125
-        grad_keys += jnp.einsum("hqk,qhd->khd", grad_scores, query_block, preferred_element_type=f32)
-        grad_values += jnp.einsum("hqk,qhd->khd", probs.astype(bf16), grad_block, preferred_element_type=f32)
-        return ((grad_keys, grad_values), grad_query.astype(bf16))
-
-    in_blocks = lambda t: t.reshape(blocks, length // blocks, heads, HD)
-    zero = jnp.zeros((length, heads, HD), f32)
-    (grad_keys, grad_values), grad_queries = lax.scan(
-        backward_block, (zero, zero), (in_blocks(q), lse, in_blocks(grad_mixed))
+    f_y = 2 if F % 2 == 0 and F <= 8 else 4
+    parts = [jnp.zeros((width,), f32)] * 2 + [
+        grad_bias_output,
+        grad_gain_one,
+        grad_shift_one,
+        grad_bias_out,
+        grad_gain_two,
+        grad_shift_two,
+    ]
+    table = jnp.stack(parts).reshape(8, F, vec).swapaxes(0, 1)
+    extra = jnp.zeros((F, 16 - 8 - fan, vec), f32).at[:, 0, :5].set(squares)
+    table = jnp.concatenate([table, grad_bias_in.reshape(F, fan, vec), extra], axis=1)
+    by_rows = lambda t: t.astype(bf16).reshape(F // f_y, f_y, t.shape[0] // F, t.shape[1])
+    input_grad, grad_qkv, grad_output, grad_in, grad_out, sums = backward(
+        S,
+        F,
+        grad_mixed,
+        q,
+        k,
+        v,
+        qt,
+        kt,
+        ot,
+        lse,
+        xfull,
+        wqkv,
+        grad_h,
+        table.reshape(F // f_y, f_y, 16, vec),
+        by_rows(grad_output),
+        by_rows(grad_in),
+        by_rows(grad_out),
     )
-    grad_q = grad_queries.reshape(length, wide)
-    grad_k = grad_keys.reshape(length, wide).astype(bf16)
-    grad_v = grad_values.reshape(length, wide).astype(bf16)
-    grads = jnp.concatenate([grad_q, grad_k, grad_v], axis=1)
-    input_part = jnp.dot(grads, wqkv.T, preferred_element_type=f32)
-    input_grad = grad_h + lax.psum_scatter(input_part, "seq", scatter_dimension=0, tiled=True)
-    grad_qkv = jnp.dot(xfull.T, grads, preferred_element_type=f32)
-
-    def over_fsdp(t):
-        return lax.psum_scatter(t, "fsdp", scatter_dimension=0, tiled=True)
-
-    wide_sums = over_fsdp(grad_qkv.astype(bf16))
-    wide_sums = lax.all_gather(wide_sums, "seq", axis=0, tiled=False).astype(f32)
+    wide = q.shape[1]
     grad_query, grad_key, grad_value = (
-        wide_sums[:, :, i * wide : (i + 1) * wide].swapaxes(0, 1).reshape(-1, width) for i in range(3)
+        grad_qkv[:, :, i * wide : (i + 1) * wide].astype(f32).swapaxes(0, 1).reshape(-1, width) for i in range(3)
     )
-    weights = [
-        lax.psum(over_fsdp(t.astype(bf16)), "seq").astype(f32) for t in (grad_output, grad_in, grad_out)
-    ]
-    bias_q = lax.all_gather(column_sums(grad_q), "seq", axis=0, tiled=True)
-    bias_v = lax.all_gather(column_sums(grad_v), "seq", axis=0, tiled=True)
-    sums = jnp.stack(
-        [
-            bias_q / S,
-            bias_v / S,
-            grad_bias_output,
-            grad_gain_one,
-            grad_shift_one,
-            grad_bias_out,
-            grad_gain_two,
-            grad_shift_two,
-        ]
-    )
-    f = lax.axis_index("fsdp")
-    extra = jnp.zeros((1, width), f32).at[0, :5].set(squares)
-    table = jnp.concatenate([sums, grad_bias_in.reshape(fan, width), extra])
-    table = lax.psum(table, ("seq", "fsdp"))
-    small_grads = lax.dynamic_slice_in_dim(table[:8], f * vec, vec, 1)
-    grad_bias_in = lax.dynamic_slice_in_dim(table[8 : 8 + fan].reshape(-1), f * vec * fan, vec * fan, 0)
-    rms = jnp.sqrt(table[8 + fan, :5] / f32(rows * width * S * F))
+    weights = [t.astype(f32) for t in (grad_output, grad_in, grad_out)]
+    small_grads = sums
+    grad_bias_in = sums[8 : 8 + fan].reshape(-1)
+    rms = jnp.sqrt(sums[8 + fan, :5] / f32(rows * width * S * F))
     return (
         layer_out.astype(bf16).reshape(layer_input.shape),
         input_grad.reshape(layer_input.shape),

time: 779 us -> 451 us (0.58)
  waiting for transfers between devices: 344 us -> 0 us
  Pallas kernels: 128 us -> 345 us
  matrix products: 148 us -> 70.6 us
  blocking collectives: 61.1 us -> 0 us
  local copies, waits for them, and re-layouts: 38 us -> 15.6 us
  other arithmetic: 29.4 us -> 11 us
  between operations: 15.1 us -> 1.49 us
    reduce_scatter x5 -> x0, waiting for transfers between devices: 283 us -> none  [the longest x4 234 us: over_fsdp(): return lax.psum_scatter(t, 'fsdp', scatter_dimension=0, tiled=True)]
    pallas_call x0 -> x1, Pallas kernels: none -> 217 us  [backward(): pl.pallas_call(functools.partial(backward_kernel, plan), out_shape=(sds((...]
    dot_general x17 -> x0, matrix products: 76.4 us -> none  [the longest x3 19 us: backward_block(): jnp.einsum('hqk,khd->qhd', grad_scores, keys, preferred_element_type=f32)]
    psum x1 -> x0, waiting for transfers between devices: 55.6 us -> none  [local(): lax.psum(over_fsdp(t.astype(bf16)), 'seq').astype(f32)]
    psum x1 -> x0, blocking collectives: 40 us -> none  [local(): table = lax.psum(table, ('seq', 'fsdp'))]
    all_gather x3 -> x0, blocking collectives: 21.1 us -> none  [the longest x1 10.4 us: local(): lax.all_gather(wide_sums, 'seq', axis=0, tiled=False).astype(f32)]
    convert_element_type x8 -> x3, other arithmetic: 18.6 us -> 3.93 us  [local(): weights = [t.astype(f32) for t in (grad_output, grad_in, grad_out)]]
  transfers between devices with their start and end apart: 7 -> 0, of which waited for: 6 -> 0; matrix products, arithmetic and copies ran while one was open for 18% -> 0% of each run, Pallas kernels for 0% -> 0%
where the time goes in v2:
time: 451 us; the launch traced here: 444 us
  Pallas kernels  345 us (76%)
  matrix products  70.6 us (16%)
  local copies, waits for them, and re-layouts  15.6 us (3%)
  other arithmetic  11 us (2%)
    pallas_call x1, Pallas kernels, backward(): pl.pallas_call(functools.partial(backward_kernel, plan), out_shape=(sds((...  217 us
    pallas_call x1, Pallas kernels, forward(): pl.pallas_call(functools.partial(forward_kernel, plan), out_shape=(sds((l...  129 us
    dot_general x1, matrix products, local(): hidden_pre = jnp.dot(normed_low, w1, preferred_element_type=f32) + bias_in  21.2 us
    dot_general x1, matrix products, local(): grad_hidden = jnp.dot(grad_branch, w2.T, preferred_element_type=f32)  13.7 us
    dot_general x1, matrix products, local(): grad_in = jnp.dot(normed_low.T, grad_pre, preferred_element_type=f32)  9.04 us
    unnamed x68, local copies, waits for them, and re-layouts  9.02 us

profile of v2, /device:TPU:25, one launch (start us, length us, event | category | flops | bytes accessed | tf_op | source)
XLA Modules:
  0.0 443.8 jit_solution(1952410916878111511)
XLA Ops:
  0.7 1.5 concatenate.16.small
  2.2 0.9 copy-done.6
  3.1 0.9 copy-done.7
  4.1 0.9 copy-done.8
  5.0 0.9 copy-done.9
  6.0 128.5 %attention_forward_and_weight_gather.1 = (bf16[1536,1024]{1,0:T(8,128)(2,1)}, bf16[1024,768]{1,0:T(8,128)(2,1)}, bf16[128,128]{1,0:T(8,128)(2,1)S(1)}, bf16[1536...) custom-call(bf16[384,1024]{1,0:T(8,128)(2,1)} %bitcast.113, ...), custom_call_target="tpu_custom_call" | custom-call | tf_op jit(solution)/shard_map/attention_forward_and_weight_gather/pallas_call | solution.py:389
  134.6 0.0 copy-start.10
  134.6 0.0 slice-start.2
  134.6 5.3 %fusion.26 = (f32[384]{0:T(512)S(1)}, f32[384,1024]{1,0:T(8,128)S(1)}, f32[]{:T(128)}, f32[]{:T(128)}) fusion(bf16[1,384,1024]{2,1,0:T(8,128)(2,1)S(1)} %copy-done.18, f32[1024]{0:T(1024)S(1)} %bitcast.136, bf16[384,1024]{1,0:T(8,128)(2,1)} %get-tuple-element.50, bf16[1024,1024]{1,0:T(8,128)(2,1)} %get-tuple-element.51), kind=kOutput, calls=%fused_computation.85 | convolution fusion | flops 808451712 | bytes 5248520 | tf_op jit(solution)/shard_map/dot_general | solution.py:956
  139.9 0.0 copy-start.13
  140.0 0.3 multiply_reduce_fusion.7
  140.3 0.2 copy-done.23
  140.5 21.2 %multiply_convert_fusion = (bf16[384,4096]{1,0:T(8,128)(2,1)S(1)}, f32[384,4096]{1,0:T(8,128)}, f32[384,4096]{1,0:T(8,128)}) fusion(f32[4096]{0:T(1024)S(1)} %bitcast.122, bf16[1024,4096]{1,0:T(8,128)(2,1)S(1)} %copy-done.23, f32[384,1024]{1,0:T(8,128)S(1)} %get-tuple-element.110, f32[1024]{0:T(1024)S(1)} %bitcast.129, f32[1024]{0:T(1024)S(1)} %bitcast.124, ...), kind=kOutput, calls=%fused_computation.6 | convolution fusion | flops 3327000576 | bytes 25717760 | tf_op jit(solution)/shard_map/dot_general | solution.py:959
  161.7 0.0 copy-start.12
  161.7 4.3 fusion.24
  166.0 0.3 multiply_reduce_fusion.6
  166.3 2.3 fusion.12
  168.6 0.6 fusion.23
  169.2 0.2 convert_reduce_fusion.2
  169.4 13.7 %convert_reduce_fusion = (f32[4096]{0:T(1024)S(1)}, bf16[384,4096]{1,0:T(8,128)(2,1)S(1)}) fusion(f32[384,4096]{1,0:T(8,128)} %get-tuple-element.108, f32[384,4096]{1,0:T(8,128)} %get-tuple-element.132, bf16[384,1024]{1,0:T(8,128)(2,1)S(1)} %get-tuple-element.96, bf16[4096,1024]{1,0:T(8,128)(2,1)} %get-tuple-element.54), kind=kOutput, calls=%fused_computation.4 | convolution fusion | flops 3246387200 | bytes 24920064 | tf_op jit(solution)/shard_map/dot_general | solution.py:972
  183.2 4.4 %multiply_reduce_fusion.4 = (f32[1024]{0:T(1024)S(1)}, f32[384]{0:T(512)S(1)}, f32[]{:T(128)}, f32[1024]{0:T(1024)S(1)}, f32[384,1024]{1,0:T(8,128)S(1)}) fusion(f32[384,1024]{1,0:T(8,128)S(1)} %get-tuple-element.110, f32[384]{0:T(512)S(1)} %fusion.16, f32[384]{0:T(512)S(1)} %broadcast_multiply_fusion.1, f32[1024]{0:T(1024)S(1)} %bitcast.126, ...), kind=kOutput, calls=%fused_computation.40 | convolution fusion | flops 3226727936 | bytes 16275460 | tf_op jit(solution)/shard_map/dot_general | solution.py:976
  187.7 0.6 fusion.22
  188.3 0.2 convert_reduce_fusion.3
  188.5 0.0 copy-start.11
  188.5 0.8 copy-done.24
  189.3 1.9 convolution_convert_fusion.3.g_o
  191.2 3.3 stack.55
  194.5 0.1 convert_reduce_fusion.1
  194.7 0.1 stack.49
  194.7 0.6 pad_maximum_fusion.table_i
  195.4 3.7 convolution_convert_fusion.2
  199.1 9.0 %convolution_convert_fusion.1 = bf16[1024,4096]{1,0:T(8,128)(2,1)} fusion(bf16[384,4096]{1,0:T(8,128)(2,1)} %copy-done.25, f32[384,1024]{1,0:T(8,128)S(1)} %copy-done.14, f32[1024]{0:T(1024)S(1)} %bitcast.132, f32[1024]{0:T(1024)S(1)} %bitcast.128, f32[384]{0:T(512)S(1)} %fusion.16, f32[384]{0:T(512)S(1)} %broadcast_multiply_fusion.1), kind=kOutput, calls=%fused_computation.2 | convolution fusion | flops 3227385856 | bytes 13118464 | tf_op jit(solution)/shard_map/dot_general | solution.py:975
  208.2 7.0 %convolution_convert_fusion = bf16[4096,1024]{1,0:T(8,128)(2,1)} fusion(bf16[384,4096]{1,0:T(8,128)(2,1)S(1)} %copy-done.27, bf16[384,1024]{1,0:T(8,128)(2,1)S(1)} %copy-done.20), kind=kOutput, calls=%fused_computation.1 | convolution fusion | flops 3225419776 | bytes 12320768 | tf_op jit(solution)/shard_map/dot_general | solution.py:971
  215.1 216.6 %attention_backward_and_gradient_sums.1 = (f32[384,1024]{1,0:T(8,128)}, bf16[4,128,768]{2,1,0:T(8,128)(2,1)}, bf16[128,1024]{1,0:T(8,128)(2,1)}, bf16[128,4096]{...) custom-call(bf16[384,1024]{1,0:T(8,128)(2,1)} %convolution_convert_fusion.3.g_o, ...), custom_call_target="tpu_custom_call" | custom-call | tf_op jit(solution)/shard_map/attention_backward_and_gradient_sums/pallas_call | solution.py:854
  431.7 1.3 convert_bitcast_fusion.1
  433.0 0.2 copy.35
  433.2 1.0 copy.38
  434.2 0.2 copy.36
  434.4 1.0 copy.39
  435.4 0.2 copy.37
  435.6 1.0 copy.40
  436.6 0.8 convert_element_type.84
  437.5 0.5 slice_bitcast_fusion.1
  438.0 1.5 convert_element_type.85
  439.5 0.6 slice_bitcast_fusion
  440.1 1.6 convert_element_type.86
  441.7 0.5 sqrt_bitcast_fusion
  442.2 1.1 copy.42
  (69 shorter events, 0.2 us)
Async XLA Ops:
  2.2 0.9 copy-start.6
  3.1 0.9 copy-start.7
  4.1 0.9 copy-start.8
  5.0 0.9 copy-start.9
  6.0 128.6 %copy-start.18 = (bf16[1,384,1024]{2,1,0:T(8,128)(2,1)S(1)}, bf16[1,384,1024]{2,1,0:T(8,128)(2,1)}, u32[]{:S(2)}) copy-start(bf16[1,384,1024]{2,1,0:T(8,128)(2,1)} %param.19) | copy-start | bytes 2359300
  134.5 5.4 %copy-start = (bf16[1536,256]{1,0:T(8,128)(2,1)}, bf16[1536,256]{1,0:T(8,128)(2,1)S(1)}, u32[]{:S(2)}) copy-start(bf16[1536,256]{1,0:T(8,128)(2,1)S(1)} %get-tuple-element.55.q_i) | copy-start | bytes 2359300
  134.5 5.4 %copy-start.1 = (bf16[1536,256]{1,0:T(8,128)(2,1)}, bf16[1536,256]{1,0:T(8,128)(2,1)S(1)}, u32[]{:S(2)}) copy-start(bf16[1536,256]{1,0:T(8,128)(2,1)S(1)} %get-tuple-element.56.k_i) | copy-start | bytes 2359300
  134.5 5.4 %copy-start.2 = (bf16[1536,256]{1,0:T(8,128)(2,1)}, bf16[1536,256]{1,0:T(8,128)(2,1)S(1)}, u32[]{:S(2)}) copy-start(bf16[1536,256]{1,0:T(8,128)(2,1)S(1)} %get-tuple-element.57.v_i) | copy-start | bytes 2359300
  134.5 5.4 %copy-start.3 = (bf16[256,1536]{1,0:T(8,128)(2,1)}, bf16[256,1536]{1,0:T(8,128)(2,1)S(1)}, u32[]{:S(2)}) copy-start(bf16[256,1536]{1,0:T(8,128)(2,1)S(1)} %get-tuple-element.58.qt_i) | copy-start | bytes 2359300
  134.5 5.4 %copy-start.4 = (bf16[256,1536]{1,0:T(8,128)(2,1)}, bf16[256,1536]{1,0:T(8,128)(2,1)S(1)}, u32[]{:S(2)}) copy-start(bf16[256,1536]{1,0:T(8,128)(2,1)S(1)} %get-tuple-element.59.kt_i) | copy-start | bytes 2359300
  134.5 5.4 %copy-start.5 = (bf16[256,1536]{1,0:T(8,128)(2,1)}, bf16[256,1536]{1,0:T(8,128)(2,1)S(1)}, u32[]{:S(2)}) copy-start(bf16[256,1536]{1,0:T(8,128)(2,1)S(1)} %get-tuple-element.60.ot_i) | copy-start | bytes 2359300
  134.6 5.4 %copy-start.10 = (f32[8,1536]{1,0:T(8,128)}, f32[8,1536]{1,0:T(8,128)S(1)}, u32[]{:S(2)}) copy-start(f32[8,1536]{1,0:T(8,128)S(1)} %get-tuple-element.61.lse_i) | copy-start | bytes 147460
  134.6 5.9 %copy-start.23 = (bf16[1024,4096]{1,0:T(8,128)(2,1)S(1)}, bf16[1024,4096]{1,0:T(8,128)(2,1)}, u32[]{:S(2)}) copy-start(bf16[1024,4096]{1,0:T(8,128)(2,1)} %get-tuple-element.53) | copy-start | bytes 25165828
  134.6 27.1 %slice-start.2 = ((s8[8388608]{0:T(1024)(128)(4,1)}), s8[4194304]{0:T(1024)(128)(4,1)S(1)}, s32[]{:S(2)}) async-start(s8[8388608]{0:T(1024)(128)(4,1)} %bitcast.149), calls=%async_computation.2 | async-start | bytes 8388608
  139.9 47.7 %copy-start.13 = (f32[384,1024]{1,0:T(8,128)}, f32[384,1024]{1,0:T(8,128)S(1)}, u32[]{:S(2)}) copy-start(f32[384,1024]{1,0:T(8,128)S(1)} %get-tuple-element.110) | copy-start | bytes 4718596
  140.5 21.2 %slice-start.3 = ((s8[8388608]{0:T(1024)(128)(4,1)}), s8[4194304]{0:T(1024)(128)(4,1)S(1)}, s32[]{:S(2)}) async-start(s8[8388608]{0:T(1024)(128)(4,1)} %bitcast.149), calls=%async_computation.3 | async-start | bytes 8388608
  161.7 4.3 copy-start.26
  161.7 4.6 %copy-start.12 = (bf16[1,384,1024]{2,1,0:T(8,128)(2,1)S(1)}, bf16[1,384,1024]{2,1,0:T(8,128)(2,1)}, u32[]{:S(2)}) copy-start(bf16[1,384,1024]{2,1,0:T(8,128)(2,1)} %param.35) | copy-start | bytes 2359300
  168.6 14.6 %slice-start = ((s8[8388608]{0:T(1024)(128)(4,1)}), s8[4194304]{0:T(1024)(128)(4,1)S(1)}, s32[]{:S(2)}) async-start(s8[8388608]{0:T(1024)(128)(4,1)} %bitcast.147), calls=%async_computation | async-start | bytes 8388608
  169.4 13.8 %copy-start.19 = (bf16[384,1024]{1,0:T(8,128)(2,1)}, bf16[384,1024]{1,0:T(8,128)(2,1)S(1)}, u32[]{:S(2)}) copy-start(bf16[384,1024]{1,0:T(8,128)(2,1)S(1)} %get-tuple-element.96) | copy-start | bytes 2359300
  169.4 13.8 %slice-start.1 = ((s8[8388608]{0:T(1024)(128)(4,1)}), s8[4194304]{0:T(1024)(128)(4,1)S(1)}, s32[]{:S(2)}) async-start(s8[8388608]{0:T(1024)(128)(4,1)} %bitcast.147), calls=%async_computation.1 | async-start | bytes 8388608
  183.2 4.5 %copy-start.25 = (bf16[384,4096]{1,0:T(8,128)(2,1)}, bf16[384,4096]{1,0:T(8,128)(2,1)S(1)}, u32[]{:S(2)}) copy-start(bf16[384,4096]{1,0:T(8,128)(2,1)S(1)} %get-tuple-element.100) | copy-start | bytes 9437188
  187.7 1.6 copy-start.24
  188.5 6.9 %copy-start.11 = (f32[384,1024]{1,0:T(8,128)}, f32[384,1024]{1,0:T(8,128)S(1)}, u32[]{:S(2)}) copy-start(f32[384,1024]{1,0:T(8,128)S(1)} %get-tuple-element.98.gh) | copy-start | bytes 4718596
  194.7 4.5 %copy-start.14 = (f32[384,1024]{1,0:T(8,128)S(1)}, f32[384,1024]{1,0:T(8,128)}, u32[]{:S(2)}) copy-start(f32[384,1024]{1,0:T(8,128)} %copy-done.13) | copy-start | bytes 4718596
  199.1 9.0 %copy-start.20 = (bf16[384,1024]{1,0:T(8,128)(2,1)S(1)}, bf16[384,1024]{1,0:T(8,128)(2,1)}, u32[]{:S(2)}) copy-start(bf16[384,1024]{1,0:T(8,128)(2,1)} %copy-done.19) | copy-start | bytes 2359300
  199.1 9.0 %copy-start.27 = (bf16[384,4096]{1,0:T(8,128)(2,1)S(1)}, bf16[384,4096]{1,0:T(8,128)(2,1)}, u32[]{:S(2)}) copy-start(bf16[384,4096]{1,0:T(8,128)(2,1)} %copy-done.26) | copy-start | bytes 9437188
  433.0 3.6 copy-start.21
  433.2 4.3 copy-start.22
  433.2 4.8 %copy-start.17 = (bf16[128,4096]{1,0:T(8,128)(2,1)S(1)}, bf16[128,4096]{1,0:T(8,128)(2,1)}, u32[]{:S(2)}) copy-start(bf16[128,4096]{1,0:T(8,128)(2,1)} %get-tuple-element.68) | copy-start | bytes 3145732
  435.4 4.7 %copy-start.16 = (bf16[512,1024]{1,0:T(8,128)(2,1)S(1)}, bf16[512,1024]{1,0:T(8,128)(2,1)}, u32[]{:S(2)}) copy-start(bf16[512,1024]{1,0:T(8,128)(2,1)} %get-tuple-element.69) | copy-start | bytes 3145732
  438.0 4.2 copy-start.15

commit v3 on v2

--- a/solution.py
+++ b/solution.py
@@ -110,11 +110,15 @@
         hi = g.hi if hi is None else hi
         return {"own": g.s, "half": c, "quarter": hi * 2 + c}[self.kind]
 
-    def start(self):
+    def start_z(self):
         g, p = self.g, self.part()
         src, dst = self.piece(p), self.place(g.f, p)
         for k in range(1, g.Z):
             rcopy(self.sems, src, dst, self.zs + k, self.ir + k, (g.s, g.zp(k))).start()
+
+    def start_y(self):
+        g, p = self.g, self.part()
+        src, dst = self.piece(p), self.place(g.f, p)
         for j in range(1, g.Y):
             rcopy(self.sems, src, dst, self.ys + j * g.Z, self.ir + j * g.Z, (g.s, g.yp(j))).start()
 
@@ -197,7 +201,8 @@
 
 def forward_kernel(plan, x, wq, wk, wv, small, wo, w1, w2, *rest):
     (xfull, wqkv, smalls, q_o, k_o, v_o, qt_o, kt_o, ot_o, lse_o, mixed, wo_f, w1_f, w2_f) = rest[:14]
-    (xs, ws, sm, qn, kn, vn, qt, kt, vt, ot, lse, oblk, onat, sems) = rest[14:]
+    (xs, ws, sm, qn, kn, vn, qt, kt, vt, ot, lse, oblk, onat, own_o, own_1, own_2, sems) = rest[14:]
+    stage = (own_o, own_1, own_2)
     S, F, rows, length, heads, wide, vec = plan.S, plan.F, plan.rows, plan.length, plan.heads, plan.wide, plan.vec
     g = Grid(S, F)
     g.greet(pltpu.get_barrier_semaphore())
@@ -222,9 +227,11 @@
             lambda p, src=src: src.at[:, pl.ds(p * wide, wide)],
             lambda o, p, col=col: ws.at[pl.ds(o * part_rows, part_rows), pl.ds(col * wide, wide)],
         )
-        item.start()
     plan.gs.bind(g, sems, lambda p: small, lambda o, p: sm.at[pl.ds(o * 16, 16)])
-    plan.gs.start()
+    first = (plan.gs, plan.gq, plan.gk, plan.gv)
+    for item in first:
+        item.start_z()
+        item.start_y()
     local.append(keep(x, mine, plan.l))
     for col, src in enumerate((wq, wk, wv)):
         local.append(
@@ -238,7 +245,7 @@
     own = []
     for i, (src, dst) in enumerate(((wo, wo_f), (w1, w1_f), (w2, w2_f))):
         n = src.shape[0]
-        own.append(keep(src, dst.at[pl.ds(g.f * n, n)], plan.l + 5 + i))
+        own.append(keep(src, stage[i], plan.l + 5 + i))
     for src, dst, (item, lo, width) in [
         (src, dst, entry)
         for src, dst, entries in ((wo, wo_f, plan.go), (w1, w1_f, plan.g1), (w2, w2_f, plan.g2))
@@ -251,8 +258,10 @@
             lambda p, src=src, lo=lo, width=width: src.at[:, pl.ds(lo + p * width, width)],
             lambda o, p, dst=dst, n=n, lo=lo, width=width: dst.at[pl.ds(o * n, n), pl.ds(lo + p * width, width)],
         )
-    big = [e[0] for e in plan.g1 + plan.go + plan.g2]
-    for item in (plan.gq, plan.gk, plan.gv, plan.gs):
+    big = [e[0] for e in plan.g1 + plan.g2[:1] + plan.go + plan.g2[1:]]
+    for item in big:
+        item.start_z()
+    for item in first:
         item.on_z()
     x_pass = []
     for m in range(1, g.H):
@@ -261,10 +270,10 @@
         copy = rcopy(sems, theirs, theirs, plan.x_s + g.H + m, plan.x_r + g.H + m, (g.sib(), g.f))
         copy.start()
         x_pass.append(copy)
-    for item in (plan.gq, plan.gk, plan.gv, plan.gs):
+    for item in big:
+        item.start_y()
+    for item in first:
         item.on_y()
-    for item in big:
-        item.start()
     rcopy(sems, mine, mine, plan.x_s, plan.x_r, (g.sib(), g.f)).wait_recv()
     for m in range(1, g.H):
         rcopy(sems, mine, mine, plan.x_s, plan.x_r + g.H + m, (g.sib(), g.f)).wait_recv()
@@ -298,6 +307,10 @@
         kt[:, pl.ds(at, rows)] = k.T.astype(bf16)
         vt[:, pl.ds(at, rows)] = v.T.astype(bf16)
 
+    for i, dst in enumerate((wo_f, w1_f, w2_f)):
+        own[i].wait()
+        n = stage[i].shape[0]
+        own[i] = keep(stage[i], dst.at[pl.ds(g.f * n, n)], plan.l + 5 + i)
     stores = [
         keep(src, dst, plan.l + 8 + i)
         for i, (src, dst) in enumerate(
@@ -306,7 +319,8 @@
     ]
     head_of = lax.broadcasted_iota(jnp.int32, (wide, rows), 0) // HD
     sent = []
-    for t in range(S):
+
+    def attend(t):
         hi = (g.hi + 1 + t // 2) % g.H
         c = (g.c + t + t // (2 * (g.H - 1))) % 2
         to = hi * 2 + c
@@ -333,16 +347,18 @@
             sent.append(copy)
         else:
             stores.append(keep(onat.at[t], dst, plan.o_s + t))
+
+    turn = 0
+    for op in plan.order:
+        if op == "T":
+            attend(turn)
+            turn += 1
+        else:
+            item = big[int(op[1:])]
+            {"z": item.on_z, "y": item.on_y, "x": item.on_x}[op[0]]()
     stores.append(keep(ot, ot_o, plan.l + 16))
     stores.append(keep(lse, lse_o, plan.l + 17))
-    for i, item in enumerate(big):
-        if i == 0:
-            item.on_z()
-        item.on_y()
-        if i + 1 < len(big):
-            big[i + 1].on_z()
-        item.on_x()
-    for item in (plan.gq, plan.gk, plan.gv, plan.gs, *big):
+    for item in (*first, *big):
         item.finish()
     for i in range(1, S):
         peer = (g.s + i) % S
@@ -372,7 +388,12 @@
     plan.go = [(Gather(alloc, S, F, Y, "half"), 0, half)]
     eighth = ff // 2 // S
     plan.g1 = [(Gather(alloc, S, F, Y, "quarter"), i * S * eighth, eighth) for i in range(2)]
-    plan.g2 = [(Gather(alloc, S, F, Y, "half"), i * half, half // 2) for i in range(2)]
+    plan.g2 = [(Gather(alloc, S, F, Y, "quarter"), 0, half // S)]
+    plan.g2 += [(Gather(alloc, S, F, Y, "half"), half + i * half // 2, half // 4) for i in range(2)]
+    plan.order = (
+        "z0", "T", "y0", "T", "z1", "T", "y1", "T", "z2", "y2", "x0", "z3", "y3", "x1", "z4", "y4",
+        "z5", "y5", "x2",
+    )
     plan.o_s, plan.o_r = alloc.take(S), alloc.take(S)
     plan.l = alloc.take(20)
     plan.sems = alloc.n
@@ -420,6 +441,9 @@
             pltpu.VMEM((8, length), f32),
             pltpu.VMEM((wide, rows), f32),
             pltpu.VMEM((S, rows, wide), bf16),
+            pltpu.VMEM(wo.shape, bf16),
+            pltpu.VMEM(w1.shape, bf16),
+            pltpu.VMEM(w2.shape, bf16),
             pltpu.SemaphoreType.DMA((plan.sems,)),
         ],
         compiler_params=pltpu.CompilerParams(collective_id=0, has_side_effects=True, vmem_limit_bytes=48 << 20),
@@ -592,12 +616,15 @@
             copy.wait_send()
         self.copy_out.wait()
 
-    def steps(self):
-        if self.kind == "half":
-            return [self.over_y, self.over_z, self.over_x_last, self.finish]
-        if self.kind == "quarter":
-            return [self.over_x_first, self.over_y, self.over_z, self.over_x_last, self.finish]
-        return [self.over_y, self.over_z, self.over_x_last, self.finish]
+    def step(self, name):
+        {
+            "D": self.over_cores,
+            "X": self.over_x_first if self.kind == "quarter" else self.over_x_last,
+            "Y": self.over_y,
+            "Z": self.over_z,
+            "L": self.over_x_last,
+            "F": self.finish,
+        }[name]()
 
 
 def backward_kernel(plan, g_o, q_i, k_i, v_i, qt_i, kt_i, ot_i, lse_i, x_i, w_i, gh, table_i, dwo, dw1, dw2, *rest):
@@ -650,7 +677,9 @@
         )
         used += n
         item.start()
-    plan.qkv.bind(g, sems, pools[used : used + 4], None, dqkv_o)
+    for i, item in enumerate(plan.qkv):
+        item.bind(g, sems, pools[used : used + 4], None, dqkv_o.at[i])
+        used += 4
     loads = [
         keep(src, dst, plan.l + i)
         for i, (src, dst) in enumerate(
@@ -671,30 +700,19 @@
         )
     ]
     items = [entry[0] for entry in plan.items]
-    for item in items:
-        item.over_cores()
-    waves = []
-    for tick in range(len(items) + 5):
-        for i, item in enumerate(items):
-            steps = item.steps()
-            if 0 <= tick - i < len(steps):
-                waves.append((tick, steps[tick - i]))
-
-    def run(upto):
-        while waves and waves[0][0] <= upto:
-            waves.pop(0)[1]()
-
     dk[...] = jnp.zeros_like(dk)
     dv[...] = jnp.zeros_like(dv)
     for copy in loads:
         copy.wait()
-    for i in range(1, S):
-        peer = (g.s + i) % S
-        recv(go.at[peer], plan.o_r + peer)
     head_of = lax.broadcasted_iota(jnp.int32, (wide, rows), 0) // HD
     head_at = lax.broadcasted_iota(jnp.int32, (rows, wide), 1) // HD
     none = jnp.zeros((), bf16)
-    for t in range(S):
+
+    def attend(t):
+        if t == 0:
+            for i in range(1, S):
+                peer = (g.s + i) % S
+                recv(go.at[peer], plan.o_r + peer)
         span = pl.ds(t * rows, rows)
         turned = go[t].astype(f32).T
         dt[...] = turned.astype(bf16)
@@ -713,29 +731,37 @@
             dk[...] += jnp.dot(ds, jnp.where(head_at == h, qn[span, :], none), preferred_element_type=f32)
             dqt[band, span] = jnp.dot(kt[band, :], ds, preferred_element_type=f32) * 0.125
 
-        run(plan.ticks[t])
-
-    sum_q = jnp.zeros((1, wide), f32)
-    sum_v = jnp.zeros((1, wide), f32)
-    for t in range(S):
-        span = pl.ds(t * rows, rows)
-        q = dqt[:, span].T.astype(bf16)
-        v = dv[span, :].astype(bf16)
-        grads[span, pl.ds(0, wide)] = q
-        grads[span, pl.ds(wide, wide)] = dk[span, :].astype(bf16)
-        grads[span, pl.ds(2 * wide, wide)] = v
-        sum_q += jnp.sum(q.astype(f32), axis=0, keepdims=True)
-        sum_v += jnp.sum(v.astype(f32), axis=0, keepdims=True)
-    Y, part_rows, width = g.Y, plan.qkv.R, xs.shape[1]
-    step = max(part_rows, 256)
-    for lo in range(0, width, step):
-        prod = lax.dot_general(
-            xs[:, pl.ds(lo, step)], grads[...], (((0,), (0,)), ((), ())), preferred_element_type=f32
-        ).astype(bf16)
-        for i in range(step // part_rows):
-            to = lo // part_rows + i
-            plan.qkv.own[0, to // Y, to % Y] = prod[i * part_rows : (i + 1) * part_rows]
-    plan.qkv.send_y()
+    totals = []
+
+    def projections(i):
+        if i == 0:
+            sum_q = jnp.zeros((1, wide), f32)
+            sum_v = jnp.zeros((1, wide), f32)
+            for t in range(S):
+                span = pl.ds(t * rows, rows)
+                q = dqt[:, span].T.astype(bf16)
+                v = dv[span, :].astype(bf16)
+                grads[span, pl.ds(0, wide)] = q
+                grads[span, pl.ds(wide, wide)] = dk[span, :].astype(bf16)
+                grads[span, pl.ds(2 * wide, wide)] = v
+                sum_q += jnp.sum(q.astype(f32), axis=0, keepdims=True)
+                sum_v += jnp.sum(v.astype(f32), axis=0, keepdims=True)
+            totals.extend((sum_q, sum_v))
+        item = plan.qkv[i]
+        part_rows, width = item.R, xs.shape[1]
+        step = max(part_rows, 256)
+        for lo in range(0, width, step):
+            prod = lax.dot_general(
+                xs[:, pl.ds(lo, step)],
+                grads[:, pl.ds(i * wide, wide)],
+                (((0,), (0,)), ((), ())),
+                preferred_element_type=f32,
+            ).astype(bf16)
+            for j in range(step // part_rows):
+                to = lo // part_rows + j
+                item.own[0, to // g.Y, to % g.Y] = prod[j * part_rows : (j + 1) * part_rows]
+        item.send_y()
+
     def part(to):
         return lax.dot_general(
             grads[pl.ds(pl.multiple_of(to * rows, rows), rows), :],
@@ -744,71 +770,95 @@
             preferred_element_type=f32,
         )
 
-    for m in [*range(1, g.H), 0]:
-        hi = (g.hi + m) % g.H
-        dx_send[m] = part(hi * 2 + 1 - g.c).astype(bf16)
-        send(dx_send.at[m], dx_core.at[m], plan.dx + m, plan.dx + g.H + m, (g.sib(), g.f))
-    for m in [*range(1, g.H), 0]:
-        hi = (g.hi + m) % g.H
-        value = part(hi * 2 + g.c)
-        recv(dx_core.at[m], plan.dx + g.H + m)
-        value += dx_core[m].astype(f32)
-        if m:
-            dx_out[m - 1] = value.astype(bf16)
-            send(dx_out.at[m - 1], dx_x.at[m - 1], plan.dx + 2 * g.H + m, plan.dx + 3 * g.H + m, (g.xp(m), g.f))
+    def input_parts():
+        for m in [*range(1, g.H), 0]:
+            hi = (g.hi + m) % g.H
+            dx_send[m] = part(hi * 2 + 1 - g.c).astype(bf16)
+            send(dx_send.at[m], dx_core.at[m], plan.dx + m, plan.dx + g.H + m, (g.sib(), g.f))
+        for m in [*range(1, g.H), 0]:
+            hi = (g.hi + m) % g.H
+            value = part(hi * 2 + g.c)
+            recv(dx_core.at[m], plan.dx + g.H + m)
+            value += dx_core[m].astype(f32)
+            if m:
+                dx_out[m - 1] = value.astype(bf16)
+                send(dx_out.at[m - 1], dx_x.at[m - 1], plan.dx + 2 * g.H + m, plan.dx + 3 * g.H + m, (g.xp(m), g.f))
+            else:
+                dx[...] += value
+
+    out = []
+
+    def input_done():
+        for m in range(1, g.H):
+            recv(dx_x.at[m - 1], plan.dx + 3 * g.H + m)
+            dx[...] += dx_x[m - 1].astype(f32)
+        out.append(keep(dx, dx_o, plan.l + 13))
+
+    def vectors(stage):
+        Y = g.Y
+        if stage == 0:
+            base = g.s * (wide // vec)
+            for i in range(wide // vec):
+                to = base + i
+                for row, value in enumerate(totals):
+                    tab[to // Y, to % Y, pl.ds(row, 1), :] = value[:, i * vec : (i + 1) * vec]
+            send(tab, tab_core, plan.t, plan.t + 1, (g.sib(), g.f))
+        if stage == 1:
+            recv(tab_core, plan.t + 1)
+            tab_x[g.hi] = tab[...] + tab_core[...]
+            for m in range(1, g.H):
+                send(tab_x.at[g.hi], tab_x.at[g.hi], plan.tx + m, plan.tx + g.H + g.hi, (g.xp(m), g.f))
+        if stage == 2:
+            for m in range(1, g.H):
+                hi = (g.hi + m) % g.H
+                recv(tab_x.at[hi], plan.tx + g.H + hi)
+            total = tab_x[0]
+            for m in range(1, g.H):
+                total += tab_x[m]
+            tab_core[...] = total
+            tab_y[g.y] = tab_core[:, g.y]
+            for j in range(1, Y):
+                y = (g.y + j) % Y
+                send(tab_core.at[:, y], tab_y.at[g.y], plan.ty + j, plan.ty + Y + g.y, (g.s, g.yp(j)))
+        if stage == 3:
+            for j in range(1, Y):
+                y = (g.y + j) % Y
+                recv(tab_y.at[y], plan.ty + Y + y)
+            total = tab_y[0]
+            for j in range(1, Y):
+                total += tab_y[j]
+            tab_s[...] = total
+            tab_z[g.z] = tab_s[g.z]
+            for k in range(1, g.Z):
+                z = (g.z + k) % g.Z
+                send(tab_s.at[z], tab_z.at[g.z], plan.tz + k, plan.tz + g.Z + g.z, (g.s, g.zp(k)))
+        if stage == 4:
+            for k in range(1, g.Z):
+                z = (g.z + k) % g.Z
+                recv(tab_z.at[z], plan.tz + g.Z + z)
+            total = tab_z[0]
+            for k in range(1, g.Z):
+                total += tab_z[k]
+            tab_y[0, 0] = total
+            out.append(keep(tab_y.at[0, 0], table_o, plan.l + 12))
+
+    named = {chr(ord("a") + i): item for i, item in enumerate(items)}
+    named.update({"q%d" % i: item for i, item in enumerate(plan.qkv)})
+    for op in plan.order:
+        what, on = op[0], op[1:]
+        if what == "T":
+            attend(int(on))
+        elif what == "G":
+            projections(int(on))
+        elif what == "I":
+            input_parts()
+        elif what == "J":
+            input_done()
+        elif what == "V":
+            vectors(int(on))
         else:
-            dx[...] += value
-    base = g.s * (wide // vec)
-    for i in range(wide // vec):
-        to = base + i
-        for row, value in ((0, sum_q), (1, sum_v)):
-            tab[to // Y, to % Y, pl.ds(row, 1), :] = value[:, i * vec : (i + 1) * vec]
-    send(tab, tab_core, plan.t, plan.t + 1, (g.sib(), g.f))
-    recv(tab_core, plan.t + 1)
-    tab_x[g.hi] = tab[...] + tab_core[...]
-    for m in range(1, g.H):
-        send(tab_x.at[g.hi], tab_x.at[g.hi], plan.tx + m, plan.tx + g.H + g.hi, (g.xp(m), g.f))
-    for m in range(1, g.H):
-        hi = (g.hi + m) % g.H
-        recv(tab_x.at[hi], plan.tx + g.H + hi)
-    total = tab_x[0]
-    for m in range(1, g.H):
-        total += tab_x[m]
-    tab_core[...] = total
-    tab_y[g.y] = tab_core[:, g.y]
-    for j in range(1, Y):
-        y = (g.y + j) % Y
-        send(tab_core.at[:, y], tab_y.at[g.y], plan.ty + j, plan.ty + Y + g.y, (g.s, g.yp(j)))
-    for j in range(1, Y):
-        y = (g.y + j) % Y
-        recv(tab_y.at[y], plan.ty + Y + y)
-    total = tab_y[0]
-    for j in range(1, Y):
-        total += tab_y[j]
-    tab_s[...] = total
-    tab_z[g.z] = tab_s[g.z]
-    for k in range(1, g.Z):
-        z = (g.z + k) % g.Z
-        send(tab_s.at[z], tab_z.at[g.z], plan.tz + k, plan.tz + g.Z + g.z, (g.s, g.zp(k)))
-    run(plan.ticks[S])
-    for k in range(1, g.Z):
-        z = (g.z + k) % g.Z
-        recv(tab_z.at[z], plan.tz + g.Z + z)
-    total = tab_z[0]
-    for k in range(1, g.Z):
-        total += tab_z[k]
-    tab_y[0, 0] = total
-    out = [keep(tab_y.at[0, 0], table_o, plan.l + 12)]
-    ending = plan.qkv.steps()
-    for i, step_of in enumerate(ending):
-        run(plan.ticks[S] + 1 + i)
-        step_of()
-    run(1000)
-    for m in range(1, g.H):
-        recv(dx_x.at[m - 1], plan.dx + 3 * g.H + m)
-        dx[...] += dx_x[m - 1].astype(f32)
-    out.append(keep(dx, dx_o, plan.l + 13))
-    for item in (*items, plan.qkv):
+            named[on].step(what)
+    for item in (*items, *plan.qkv):
         item.done()
     for copy in sent:
         copy.wait_send()
@@ -827,14 +877,20 @@
     R, R2 = width // F, ff // F
     ones = [(Reduce(alloc, S, F, Y, R, width, "quarter"), "1", i * width, 0) for i in range(ff // width)]
     twos = [(Reduce(alloc, S, F, Y, R2 // 4, width, "half"), "2", 0, i * (R2 // 4)) for i in range(4)]
-    plan.items = [e for pair in zip(twos, ones) for e in pair]
+    plan.items = [e for pair in zip(ones, twos) for e in pair]
     plan.items.append((Reduce(alloc, S, F, Y, R, width, "half"), "o", 0, 0))
-    plan.qkv = Reduce(alloc, S, F, Y, R, 3 * plan.wide, "own")
+    plan.qkv = [Reduce(alloc, S, F, Y, R, plan.wide, "own") for _ in range(3)]
     plan.o_s, plan.o_r = alloc.take(S), alloc.take(S)
     plan.dx = alloc.take(4 * S)
     plan.t, plan.tx, plan.ty, plan.tz = alloc.take(2), alloc.take(S), alloc.take(2 * Y), alloc.take(2 * F // Y)
     plan.l = alloc.take(14)
-    plan.ticks = [1, 3, 5, 7, 9]
+    plan.order = (
+        "Da", "Db", "Dc", "Dd", "T0", "Df", "De", "Yb", "T1", "Xa", "T2", "Dg", "Yd", "Dh", "Zb", "Xc",
+        "T3", "Yf", "G0", "Xe", "Ya", "Zd", "G1", "G2", "I", "Xg", "V0", "Yh", "Xb", "Zf", "V1", "Fb",
+        "Xd", "Fd", "Yc", "Za", "Yq0", "Ye", "Di", "Zh", "J", "Yq1", "Xf", "Zc", "V2", "Ff", "La", "Fa",
+        "Yq2", "Xh", "Zq0", "Lc", "Fh", "Fc", "Lq0", "Yg", "Fq0", "Ze", "Le", "Fe", "Zq1", "Lq1", "Yi", "Fq1",
+        "V3", "Zq2", "Lq2", "Fq2", "Zg", "Lg", "Fg", "Zi", "V4", "Xi", "Fi",
+    )
     plan.sems = alloc.n
     return plan
 
@@ -850,12 +906,12 @@
     R, R2 = width // F, ff // F
     sds = jax.ShapeDtypeStruct
     any_ = pl.BlockSpec(memory_space=pl.ANY)
-    pools = [s for e in plan.items for s in e[0].shapes] + plan.qkv.shapes
+    pools = [s for e in plan.items for s in e[0].shapes] + [s for i in plan.qkv for s in i.shapes]
     return pl.pallas_call(
         functools.partial(backward_kernel, plan),
         out_shape=(
             sds((rows, width), f32),
-            sds((S, R, 3 * wide), bf16),
+            sds((3, S, R, wide), bf16),
             sds((R, width), bf16),
             sds((R, ff), bf16),
             sds((R2, width), bf16),
@@ -1013,7 +1069,7 @@
     )
     wide = q.shape[1]
     grad_query, grad_key, grad_value = (
-        grad_qkv[:, :, i * wide : (i + 1) * wide].astype(f32).swapaxes(0, 1).reshape(-1, width) for i in range(3)
+        t.astype(f32).swapaxes(0, 1).reshape(-1, width) for t in grad_qkv
     )
     weights = [t.astype(f32) for t in (grad_output, grad_in, grad_out)]
     small_grads = sums

time: 451 us -> 369 us (0.82)
  the two profiles are of different devices: /device:TPU:25 before, /device:TPU:9 now
where the time goes in v3:
time: 369 us; the launch traced here: 362 us
  Pallas kernels  263 us (71%)
  matrix products  70.6 us (19%)
  local copies, waits for them, and re-layouts  15.6 us (4%)
  other arithmetic  11 us (3%)
    pallas_call x1, Pallas kernels, backward(): pl.pallas_call(functools.partial(backward_kernel, plan), out_shape=(sds((...  142 us
    pallas_call x1, Pallas kernels, forward(): pl.pallas_call(functools.partial(forward_kernel, plan), out_shape=(sds((l...  121 us
    dot_general x1, matrix products, local(): hidden_pre = jnp.dot(normed_low, w1, preferred_element_type=f32) + bias_in  21.2 us
    dot_general x1, matrix products, local(): grad_hidden = jnp.dot(grad_branch, w2.T, preferred_element_type=f32)  13.7 us
    dot_general x1, matrix products, local(): grad_in = jnp.dot(normed_low.T, grad_pre, preferred_element_type=f32)  9.04 us
    unnamed x68, local copies, waits for them, and re-layouts  9.03 us

profile of v3, /device:TPU:9, one launch (start us, length us, event | category | flops | bytes accessed | tf_op | source)
XLA Modules:
  0.0 361.6 jit_solution(1673090139586744085)
XLA Ops:
  0.7 1.5 concatenate.16.small
  2.2 0.9 copy-done.6
  3.1 0.9 copy-done.7
  4.1 0.9 copy-done.8
  5.0 0.9 copy-done.9
  6.0 121.0 %attention_forward_and_weight_gather.1 = (bf16[1536,1024]{1,0:T(8,128)(2,1)}, bf16[1024,768]{1,0:T(8,128)(2,1)}, bf16[128,128]{1,0:T(8,128)(2,1)S(1)}, bf16[1536...) custom-call(bf16[384,1024]{1,0:T(8,128)(2,1)} %bitcast.122, ...), custom_call_target="tpu_custom_call" | custom-call | tf_op jit(solution)/shard_map/attention_forward_and_weight_gather/pallas_call | solution.py:410
  127.0 0.0 copy-start.10
  127.1 0.0 slice-start.2
  127.1 5.3 %fusion.26 = (f32[384]{0:T(512)S(1)}, f32[384,1024]{1,0:T(8,128)S(1)}, f32[]{:T(128)}, f32[]{:T(128)}) fusion(bf16[1,384,1024]{2,1,0:T(8,128)(2,1)S(1)} %copy-done.18, f32[1024]{0:T(1024)S(1)} %bitcast.145, bf16[384,1024]{1,0:T(8,128)(2,1)} %get-tuple-element.50, bf16[1024,1024]{1,0:T(8,128)(2,1)} %get-tuple-element.51), kind=kOutput, calls=%fused_computation.85 | convolution fusion | flops 808451712 | bytes 5248520 | tf_op jit(solution)/shard_map/dot_general | solution.py:1012
  132.4 0.0 copy-start.13
  132.4 0.3 multiply_reduce_fusion.7
  132.7 0.2 copy-done.23
  132.9 21.2 %multiply_convert_fusion = (bf16[384,4096]{1,0:T(8,128)(2,1)S(1)}, f32[384,4096]{1,0:T(8,128)}, f32[384,4096]{1,0:T(8,128)}) fusion(f32[4096]{0:T(1024)S(1)} %bitcast.131, bf16[1024,4096]{1,0:T(8,128)(2,1)S(1)} %copy-done.23, f32[384,1024]{1,0:T(8,128)S(1)} %get-tuple-element.110, f32[1024]{0:T(1024)S(1)} %bitcast.138, f32[1024]{0:T(1024)S(1)} %bitcast.133, ...), kind=kOutput, calls=%fused_computation.6 | convolution fusion | flops 3327000576 | bytes 25717760 | tf_op jit(solution)/shard_map/dot_general | solution.py:1015
  154.1 0.0 copy-start.12
  154.2 4.3 %fusion.24 = (f32[384]{0:T(512)S(1)}, f32[384,1024]{1,0:T(8,128)S(1)}, f32[]{:T(128)}) fusion(f32[1024]{0:T(1024)S(1)} %bitcast.144, f32[1024]{0:T(1024)S(1)} %bitcast.139, f32[1024]{0:T(1024)S(1)} %bitcast.134, f32[384]{0:T(512)S(1)} %fusion.16, f32[384,1024]{1,0:T(8,128)S(1)} %get-tuple-element.110, f32[384]{0:T(512)S(1)} %broadcast_multiply_fusion.1, ...), kind=kOutput, calls=%fused_computation.84 | convolution fusion | flops 3224763904 | bytes 14696964 | tf_op jit(solution)/shard_map/dot_general | solution.py:1018
  158.4 0.3 multiply_reduce_fusion.6
  158.7 2.3 fusion.12
  161.1 0.6 fusion.23
  161.7 0.2 convert_reduce_fusion.2
  161.9 13.7 %convert_reduce_fusion = (f32[4096]{0:T(1024)S(1)}, bf16[384,4096]{1,0:T(8,128)(2,1)S(1)}) fusion(f32[384,4096]{1,0:T(8,128)} %get-tuple-element.108, f32[384,4096]{1,0:T(8,128)} %get-tuple-element.132, bf16[384,1024]{1,0:T(8,128)(2,1)S(1)} %get-tuple-element.96, bf16[4096,1024]{1,0:T(8,128)(2,1)} %get-tuple-element.54), kind=kOutput, calls=%fused_computation.4 | convolution fusion | flops 3246387200 | bytes 24920064 | tf_op jit(solution)/shard_map/dot_general | solution.py:1028
  175.7 4.4 %multiply_reduce_fusion.4 = (f32[1024]{0:T(1024)S(1)}, f32[384]{0:T(512)S(1)}, f32[]{:T(128)}, f32[1024]{0:T(1024)S(1)}, f32[384,1024]{1,0:T(8,128)S(1)}) fusion(f32[384,1024]{1,0:T(8,128)S(1)} %get-tuple-element.110, f32[384]{0:T(512)S(1)} %fusion.16, f32[384]{0:T(512)S(1)} %broadcast_multiply_fusion.1, f32[1024]{0:T(1024)S(1)} %bitcast.135, ...), kind=kOutput, calls=%fused_computation.40 | convolution fusion | flops 3226727936 | bytes 16275460 | tf_op jit(solution)/shard_map/dot_general | solution.py:1032
  180.1 0.6 fusion.22
  180.7 0.2 convert_reduce_fusion.3
  180.9 0.0 copy-start.11
  181.0 0.8 copy-done.24
  181.7 1.9 convolution_convert_fusion.3.g_o
  183.7 3.3 stack.55
  187.0 0.1 convert_reduce_fusion.1
  187.1 0.1 stack.49
  187.2 0.6 pad_maximum_fusion.table_i
  187.8 3.7 %convolution_convert_fusion.2 = bf16[1024,1024]{1,0:T(8,128)(2,1)} fusion(bf16[384,1024]{1,0:T(8,128)(2,1)} %get-tuple-element.50, f32[384,1024]{1,0:T(8,128)S(1)} %get-tuple-element.98.gh), kind=kOutput, calls=%fused_computation.29 | convolution fusion | flops 806748160 | bytes 4456448 | tf_op jit(solution)/shard_map/dot_general | solution.py:1036
  191.6 9.0 %convolution_convert_fusion.1 = bf16[1024,4096]{1,0:T(8,128)(2,1)} fusion(bf16[384,4096]{1,0:T(8,128)(2,1)} %copy-done.25, f32[384,1024]{1,0:T(8,128)S(1)} %copy-done.14, f32[1024]{0:T(1024)S(1)} %bitcast.141, f32[1024]{0:T(1024)S(1)} %bitcast.137, f32[384]{0:T(512)S(1)} %fusion.16, f32[384]{0:T(512)S(1)} %broadcast_multiply_fusion.1), kind=kOutput, calls=%fused_computation.2 | convolution fusion | flops 3227385856 | bytes 13118464 | tf_op jit(solution)/shard_map/dot_general | solution.py:1031
  200.6 7.0 %convolution_convert_fusion = bf16[4096,1024]{1,0:T(8,128)(2,1)} fusion(bf16[384,4096]{1,0:T(8,128)(2,1)S(1)} %copy-done.27, bf16[384,1024]{1,0:T(8,128)(2,1)S(1)} %copy-done.20), kind=kOutput, calls=%fused_computation.1 | convolution fusion | flops 3225419776 | bytes 12320768 | tf_op jit(solution)/shard_map/dot_general | solution.py:1027
  207.6 141.9 %attention_backward_and_gradient_sums.1 = (f32[384,1024]{1,0:T(8,128)}, bf16[3,4,128,256]{3,2,1,0:T(8,128)(2,1)}, bf16[128,1024]{1,0:T(8,128)(2,1)}, bf16[128,40...) custom-call(bf16[384,1024]{1,0:T(8,128)(2,1)} %convolution_convert_fusion.3.g_o, ...), custom_call_target="tpu_custom_call" | custom-call | tf_op jit(solution)/shard_map/attention_backward_and_gradient_sums/pallas_call | solution.py:910
  349.5 1.3 convert_bitcast_fusion.1
  350.8 0.2 copy.35
  351.0 1.0 copy.38
  352.0 0.2 copy.36
  352.2 1.0 copy.39
  353.2 0.2 copy.37
  353.4 1.0 copy.40
  354.4 0.8 convert_element_type.96
  355.3 0.5 slice_bitcast_fusion.1
  355.8 1.5 convert_element_type.97
  357.3 0.6 slice_bitcast_fusion
  357.9 1.6 convert_element_type.98
  359.5 0.5 sqrt_bitcast_fusion
  360.0 1.1 copy.42
  (69 shorter events, 0.2 us)
Async XLA Ops:
  2.2 0.9 copy-start.6
  3.1 0.9 copy-start.7
  4.1 0.9 copy-start.8
  5.0 0.9 copy-start.9
  6.0 121.1 %copy-start.18 = (bf16[1,384,1024]{2,1,0:T(8,128)(2,1)S(1)}, bf16[1,384,1024]{2,1,0:T(8,128)(2,1)}, u32[]{:S(2)}) copy-start(bf16[1,384,1024]{2,1,0:T(8,128)(2,1)} %param.19) | copy-start | bytes 2359300
  127.0 5.4 %copy-start = (bf16[1536,256]{1,0:T(8,128)(2,1)}, bf16[1536,256]{1,0:T(8,128)(2,1)S(1)}, u32[]{:S(2)}) copy-start(bf16[1536,256]{1,0:T(8,128)(2,1)S(1)} %get-tuple-element.55.q_i) | copy-start | bytes 2359300
  127.0 5.4 %copy-start.1 = (bf16[1536,256]{1,0:T(8,128)(2,1)}, bf16[1536,256]{1,0:T(8,128)(2,1)S(1)}, u32[]{:S(2)}) copy-start(bf16[1536,256]{1,0:T(8,128)(2,1)S(1)} %get-tuple-element.56.k_i) | copy-start | bytes 2359300
  127.0 5.4 %copy-start.2 = (bf16[1536,256]{1,0:T(8,128)(2,1)}, bf16[1536,256]{1,0:T(8,128)(2,1)S(1)}, u32[]{:S(2)}) copy-start(bf16[1536,256]{1,0:T(8,128)(2,1)S(1)} %get-tuple-element.57.v_i) | copy-start | bytes 2359300
  127.0 5.4 %copy-start.3 = (bf16[256,1536]{1,0:T(8,128)(2,1)}, bf16[256,1536]{1,0:T(8,128)(2,1)S(1)}, u32[]{:S(2)}) copy-start(bf16[256,1536]{1,0:T(8,128)(2,1)S(1)} %get-tuple-element.58.qt_i) | copy-start | bytes 2359300
  127.0 5.4 %copy-start.4 = (bf16[256,1536]{1,0:T(8,128)(2,1)}, bf16[256,1536]{1,0:T(8,128)(2,1)S(1)}, u32[]{:S(2)}) copy-start(bf16[256,1536]{1,0:T(8,128)(2,1)S(1)} %get-tuple-element.59.kt_i) | copy-start | bytes 2359300
  127.0 5.4 %copy-start.5 = (bf16[256,1536]{1,0:T(8,128)(2,1)}, bf16[256,1536]{1,0:T(8,128)(2,1)S(1)}, u32[]{:S(2)}) copy-start(bf16[256,1536]{1,0:T(8,128)(2,1)S(1)} %get-tuple-element.60.ot_i) | copy-start | bytes 2359300
  127.0 5.4 %copy-start.10 = (f32[8,1536]{1,0:T(8,128)}, f32[8,1536]{1,0:T(8,128)S(1)}, u32[]{:S(2)}) copy-start(f32[8,1536]{1,0:T(8,128)S(1)} %get-tuple-element.61.lse_i) | copy-start | bytes 147460
  127.1 5.9 %copy-start.23 = (bf16[1024,4096]{1,0:T(8,128)(2,1)S(1)}, bf16[1024,4096]{1,0:T(8,128)(2,1)}, u32[]{:S(2)}) copy-start(bf16[1024,4096]{1,0:T(8,128)(2,1)} %get-tuple-element.53) | copy-start | bytes 25165828
  127.1 27.0 %slice-start.2 = ((s8[8388608]{0:T(1024)(128)(4,1)}), s8[4194304]{0:T(1024)(128)(4,1)S(1)}, s32[]{:S(2)}) async-start(s8[8388608]{0:T(1024)(128)(4,1)} %bitcast.158), calls=%async_computation.2 | async-start | bytes 8388608
  132.4 47.7 %copy-start.13 = (f32[384,1024]{1,0:T(8,128)}, f32[384,1024]{1,0:T(8,128)S(1)}, u32[]{:S(2)}) copy-start(f32[384,1024]{1,0:T(8,128)S(1)} %get-tuple-element.110) | copy-start | bytes 4718596
  132.9 21.2 %slice-start.3 = ((s8[8388608]{0:T(1024)(128)(4,1)}), s8[4194304]{0:T(1024)(128)(4,1)S(1)}, s32[]{:S(2)}) async-start(s8[8388608]{0:T(1024)(128)(4,1)} %bitcast.158), calls=%async_computation.3 | async-start | bytes 8388608
  154.1 4.3 %copy-start.26 = (bf16[384,4096]{1,0:T(8,128)(2,1)}, bf16[384,4096]{1,0:T(8,128)(2,1)S(1)}, u32[]{:S(2)}) copy-start(bf16[384,4096]{1,0:T(8,128)(2,1)S(1)} %get-tuple-element.107) | copy-start | bytes 9437188
  154.1 4.6 %copy-start.12 = (bf16[1,384,1024]{2,1,0:T(8,128)(2,1)S(1)}, bf16[1,384,1024]{2,1,0:T(8,128)(2,1)}, u32[]{:S(2)}) copy-start(bf16[1,384,1024]{2,1,0:T(8,128)(2,1)} %param.35) | copy-start | bytes 2359300
  161.1 14.6 %slice-start = ((s8[8388608]{0:T(1024)(128)(4,1)}), s8[4194304]{0:T(1024)(128)(4,1)S(1)}, s32[]{:S(2)}) async-start(s8[8388608]{0:T(1024)(128)(4,1)} %bitcast.156), calls=%async_computation | async-start | bytes 8388608
  161.9 13.8 %copy-start.19 = (bf16[384,1024]{1,0:T(8,128)(2,1)}, bf16[384,1024]{1,0:T(8,128)(2,1)S(1)}, u32[]{:S(2)}) copy-start(bf16[384,1024]{1,0:T(8,128)(2,1)S(1)} %get-tuple-element.96) | copy-start | bytes 2359300
  161.9 13.8 %slice-start.1 = ((s8[8388608]{0:T(1024)(128)(4,1)}), s8[4194304]{0:T(1024)(128)(4,1)S(1)}, s32[]{:S(2)}) async-start(s8[8388608]{0:T(1024)(128)(4,1)} %bitcast.156), calls=%async_computation.1 | async-start | bytes 8388608
  175.6 4.5 %copy-start.25 = (bf16[384,4096]{1,0:T(8,128)(2,1)}, bf16[384,4096]{1,0:T(8,128)(2,1)S(1)}, u32[]{:S(2)}) copy-start(bf16[384,4096]{1,0:T(8,128)(2,1)S(1)} %get-tuple-element.100) | copy-start | bytes 9437188
  180.1 1.6 copy-start.24
  180.9 6.9 %copy-start.11 = (f32[384,1024]{1,0:T(8,128)}, f32[384,1024]{1,0:T(8,128)S(1)}, u32[]{:S(2)}) copy-start(f32[384,1024]{1,0:T(8,128)S(1)} %get-tuple-element.98.gh) | copy-start | bytes 4718596
  187.1 4.5 %copy-start.14 = (f32[384,1024]{1,0:T(8,128)S(1)}, f32[384,1024]{1,0:T(8,128)}, u32[]{:S(2)}) copy-start(f32[384,1024]{1,0:T(8,128)} %copy-done.13) | copy-start | bytes 4718596
  191.6 9.0 %copy-start.20 = (bf16[384,1024]{1,0:T(8,128)(2,1)S(1)}, bf16[384,1024]{1,0:T(8,128)(2,1)}, u32[]{:S(2)}) copy-start(bf16[384,1024]{1,0:T(8,128)(2,1)} %copy-done.19) | copy-start | bytes 2359300
  191.6 9.0 %copy-start.27 = (bf16[384,4096]{1,0:T(8,128)(2,1)S(1)}, bf16[384,4096]{1,0:T(8,128)(2,1)}, u32[]{:S(2)}) copy-start(bf16[384,4096]{1,0:T(8,128)(2,1)} %copy-done.26) | copy-start | bytes 9437188
  350.8 3.6 %copy-start.21 = (bf16[128,1024]{1,0:T(8,128)(2,1)S(1)}, bf16[128,1024]{1,0:T(8,128)(2,1)}, u32[]{:S(2)}) copy-start(bf16[128,1024]{1,0:T(8,128)(2,1)} %get-tuple-element.66) | copy-start | bytes 786436
  351.0 4.3 %copy-start.22 = (f32[16,128]{1,0:T(8,128)S(1)}, f32[16,128]{1,0:T(8,128)}, u32[]{:S(2)}) copy-start(f32[16,128]{1,0:T(8,128)} %get-tuple-element.67) | copy-start | bytes 24580
  351.0 4.8 %copy-start.17 = (bf16[128,4096]{1,0:T(8,128)(2,1)S(1)}, bf16[128,4096]{1,0:T(8,128)(2,1)}, u32[]{:S(2)}) copy-start(bf16[128,4096]{1,0:T(8,128)(2,1)} %get-tuple-element.68) | copy-start | bytes 3145732
  353.2 4.7 %copy-start.16 = (bf16[512,1024]{1,0:T(8,128)(2,1)S(1)}, bf16[512,1024]{1,0:T(8,128)(2,1)}, u32[]{:S(2)}) copy-start(bf16[512,1024]{1,0:T(8,128)(2,1)} %get-tuple-element.69) | copy-start | bytes 3145732
  355.8 4.2 %copy-start.15 = (f32[384,1024]{1,0:T(8,128)S(1)}, f32[384,1024]{1,0:T(8,128)}, u32[]{:S(2)}) copy-start(f32[384,1024]{1,0:T(8,128)} %get-tuple-element.64) | copy-start | bytes 4718596
